TPU v7x, 32 devices: a whole 2x2x4 slice. The times are simulated.
32 devices in a mesh: gx: 8 (over y, x, core), gy: 4 (over z).
Axes of the slice: x: 2, y: 2, z: 4, core: 2. Of those that a mesh axis runs over, the one named last changes fastest.
Arguments:
- scalar: float32 [512, 256, 512], P('gx', 'gy'), may hold values from -6 to 6
- prefactor: float32 [512, 256, 512], P('gx', 'gy'), may hold values from 0.05 to 1
- factor_x: float32 [512, 512], P('gx'), may hold values from -0.375 to 0.375
- factor_y: float32 [256, 64], P('gy'), may hold values from -0.5 to 0.5
- factor_z: bfloat16 [512, 128], replicated, may hold values from -0.25 to 0.25
Outputs:
- advanced: float32 [512, 256, 512], P('gx', 'gy')
- core: float32 [512, 64, 128], P('gx', 'gy')
All inputs are finite; a program needn't handle non-finite values.
Results may differ from a plain program's by a relative error of at most 0.0029.
Values sent between devices are 32-bit elements; how exact they have to be, the bound alone decides.
No kernel may reach another device: no remote copies, remote signals or barrier semaphores. Data moves between devices by JAX's collectives and lax.ppermute only.
A program may use at most 128 MiB of HBM per device.

v0:
```python
import jax
import jax.numpy as jnp
from jax import lax
from jax.sharding import PartitionSpec as P

spread_rate = 0.12
activation = 2.0


def extended(array, sides, width):
    for axis, dim in sides:
        peers, length = (lax.axis_size(axis), array.shape[dim])
        up = [(i, (i + 1) % peers) for i in range(peers - 1)]
        down = [(j, i) for i, j in up]
        last = lax.slice_in_dim(array, length - width, length, axis=dim)
        first = lax.slice_in_dim(array, 0, width, axis=dim)
        before = lax.ppermute(last, axis, up)
        after = lax.ppermute(first, axis, down)
        array = jnp.concatenate([before, array, after], axis=dim)
    return array


def laplace(padded):
    center = padded[1:-1, 1:-1]
    z_padded = jnp.pad(center, ((0, 0), (0, 0), (1, 1)))
    beside = padded[2:, 1:-1] + padded[:-2, 1:-1] + padded[1:-1, 2:] + padded[1:-1, :-2]
    beside = beside + z_padded[:, :, 2:] + z_padded[:, :, :-2]
    return beside - 6.0 * center


def sources(field, prefactor):
    return prefactor * jnp.exp(-activation / (1.0 + field * field))


def section_rate(field, prefactor):
    padded = extended(field, (("gx", 0), ("gy", 1)), 1)
    return spread_rate * laplace(padded) + sources(field, prefactor)


def on_device(scalar, prefactor, factor_x, factor_y, factor_z):
    cells_x, cells_y, depth = scalar.shape
    first = section_rate(scalar, prefactor)
    middle = scalar + first
    second = section_rate(middle, prefactor)
    advanced = scalar + 0.5 * (first + second)
    lowered = advanced.astype(jnp.bfloat16)
    z_reduced = jnp.dot(
        lowered.reshape(cells_x * cells_y, depth), factor_z, preferred_element_type=jnp.float32
    ).reshape(cells_x, cells_y, -1)
    y_reduced = jnp.einsum("xyc,yb->xbc", z_reduced, factor_y, precision=lax.Precision.HIGHEST)
    y_owned = lax.psum_scatter(y_reduced, "gy", scatter_dimension=1, tiled=True)
    core = lax.psum_scatter(
        jnp.einsum("xa,xbc->abc", factor_x, y_owned, precision=lax.Precision.HIGHEST),
        "gx",
        scatter_dimension=0,
        tiled=True,
    )
    return (advanced, core)


def solution(mesh):
    return jax.shard_map(
        on_device,
        mesh=mesh,
        in_specs=(P("gx", "gy", None), P("gx", "gy", None), P("gx", None), P("gy", None), P()),
        out_specs=(P("gx", "gy", None), P("gx", "gy", None)),
        check_vma=False,
    )
```

profile of v0, /device:TPU:0, one launch (start us, length us, event | category | flops | bytes accessed | tf_op | source)
XLA Modules:
  0.0 266.1 jit_solution(18289151379626399568)
XLA Ops:
  7.2 1.0 fusion.29
  8.2 2.4 collective-permute-start.1
  10.7 1.3 collective-permute-start
  12.0 8.2 %copy.43 = f32[64,64,512]{2,0,1:T(8,128)S(1)} copy(f32[64,64,512]{2,1,0:T(8,128)} %param.5) | data formatting | bytes 16777216 | tf_op args[0]
  20.5 3.1 %copy-done.1 = f32[64,64,512]{2,0,1:T(8,128)} copy-done((f32[64,64,512]{2,0,1:T(8,128)}, f32[64,64,512]{2,0,1:T(8,128)S(1)}, u32[]{:S(2)}) %copy-start.1) | copy-done | bytes 8388632
  23.6 1.3 collective-permute-start.2
  24.9 5.1 %collective-permute-start.3 = (f32[66,1,512]{2,0,1:T(8,128)S(1)}, f32[66,1,512]{2,0,1:T(8,128)S(1)}, u32[]{:S(2)}, u32[]{:S(2)}) collective-permute-start(f32[66,1,512]{2,0,1:T(8,128)S(1)} %get-tuple-element.15), channel_id=1, source_target_pairs={{0,1},{1,2},{2,3},{4,5},{5,6},{6,7},{8,9},{9,10},{10,11},{12,13},{... | collective-permute-start | bytes 405512 | tf_op jit(solution)/shard_map/ppermute | solution.py:17
  31.1 1.5 collective-permute-done.3
  32.5 42.2 %copy_add_fusion = (f32[64,64,512]{2,0,1:T(8,128)}, f32[64,64,512]{2,0,1:T(8,128)}) fusion(f32[64,64,512]{2,1,0:T(8,128)} %param.5, f32[64,64,512]{2,0,1:T(8,128)} %copy-done.1, f32[64,64,512]{2,1,0:T(8,128)} %param.6, f32[1,64,512]{2,0,1:T(1,128)S(1)} %copy.24, f32[1,64,512]{2,0,1:T(1,128)S(1)} %copy.25, f32[66,1,512]{2,0,1:T(8,128)S(1)} %collective-permute-done.3, ...), kind=kLoop, calls=%fused_computation.53 | loop fusion | flops 46137344 | bytes 42475520 | tf_op jit(solution)/shard_map/add | solution.py:43
  74.7 1.8 fusion.28
  76.6 1.3 collective-permute-start.4
  77.9 4.2 %collective-permute-start.5 = (f32[1,64,512]{2,1,0:T(8,128)S(1)}, f32[1,64,512]{2,1,0:T(8,128)S(1)}, u32[]{:S(2)}, u32[]{:S(2)}) collective-permute-start(f32[1,64,512]{2,1,0:T(8,128)S(1)} %copy.38), channel_id=1, source_target_pairs={{0,4},{4,8},{8,12},{12,16},{16,20},{20,24},{24,28},{1,5},{5,9},{9,... | collective-permute-start | bytes 393224 | tf_op jit(solution)/shard_map/ppermute | solution.py:17
  83.2 1.0 pad_maximum_fusion.18
  84.2 1.3 collective-permute-start.6
  85.5 4.9 %collective-permute-start.7 = (f32[66,1,512]{2,0,1:T(8,128)S(1)}, f32[66,1,512]{2,0,1:T(8,128)S(1)}, u32[]{:S(2)}, u32[]{:S(2)}) collective-permute-start(f32[66,1,512]{2,0,1:T(8,128)S(1)} %get-tuple-element.13), channel_id=1, source_target_pairs={{0,1},{1,2},{2,3},{4,5},{5,6},{6,7},{8,9},{9,10},{10,11},{12,13},{... | collective-permute-start | bytes 405512 | tf_op jit(solution)/shard_map/ppermute | solution.py:17
  91.4 1.5 collective-permute-done.7
  92.9 44.1 %fusion.25 = (bf16[64,64,512]{2,0,1:T(8,128)(2,1)S(1)}, f32[64,64,512]{2,0,1:T(8,128)}) fusion(f32[64,64,512]{2,0,1:T(8,128)} %get-tuple-element.11, f32[64,64,512]{2,0,1:T(8,128)} %get-tuple-element.10, f32[64,64,512]{2,1,0:T(8,128)} %param.6, f32[1,64,512]{2,0,1:T(1,128)S(1)} %copy.37, f32[1,64,512]{2,0,1:T(1,128)S(1)} %copy.39, ...), kind=kLoop, calls=%fused_computation.54 | loop fusion | flops 52428800 | bytes 46669824 | tf_op jit(solution)/shard_map/convert_element_type | solution.py:46
  137.0 4.7 %fusion.19 = f32[64,64,128]{2,1,0:T(8,128)S(1)} fusion(bf16[64,64,512]{2,0,1:T(8,128)(2,1)S(1)} %get-tuple-element.8, bf16[512,128]{1,0:T(8,128)(2,1)S(1)} %copy-done.3), kind=kOutput, calls=%fused_computation.39 | convolution fusion | flops 536870912 | bytes 6422528 | tf_op jit(solution)/shard_map/dot_general | solution.py:47
  141.6 3.3 %convolution_bitcast_fusion.1 = f32[64,64,128]{2,1,0:T(8,128)} fusion(f32[64,64,128]{2,1,0:T(8,128)S(1)} %fusion.19, f32[64,64]{1,0:T(8,128)S(1)} %copy-done.2), kind=kOutput, calls=%fused_computation.42 | convolution fusion | flops 402653184 | bytes 4210688 | tf_op jit(solution)/shard_map/xyc,yb->xbc/dot_general | solution.py:50
  145.0 52.1 %reduce-scatter.3.cloned.1.call-done = f32[64,16,128]{2,1,0:T(8,128)} async-done(((f32[64,64,128]{2,1,0:T(8,128)}), f32[64,16,128]{2,1,0:T(8,128)}) %reduce-scatter.3.cloned.1.call-update) | async-done | bytes 524304 | tf_op jit(solution)/shard_map/reduce_scatter | solution.py:51
  197.2 6.1 %convolution_bitcast_fusion = f32[512,16,128]{0,2,1:T(8,128)} fusion(f32[64,16,128]{2,1,0:T(8,128)} %reduce-scatter.3.cloned.1.call-done, f32[64,512]{1,0:T(8,128)S(1)} %copy-done), kind=kOutput, calls=%fused_computation.41 | convolution fusion | flops 805306368 | bytes 4849664 | tf_op jit(solution)/shard_map/xa,xbc->abc/dot_general | solution.py:53
  203.2 5.5 %copy.47 = f32[512,16,128]{2,1,0:T(8,128)} copy(f32[512,16,128]{0,2,1:T(8,128)} %convolution_bitcast_fusion) | data formatting | bytes 8388608 | tf_op jit(solution)/shard_map/xa,xbc->abc/dot_general | solution.py:53
  208.7 11.9 %copy.48 = f32[64,64,512]{2,1,0:T(8,128)} copy(f32[64,64,512]{2,0,1:T(8,128)} %get-tuple-element.9) | data formatting | bytes 16777216
  220.6 38.6 %reduce-scatter.5.cloned.1.call-done = f32[64,16,128]{2,1,0:T(8,128)} async-done(((f32[512,16,128]{2,1,0:T(8,128)}), f32[64,16,128]{2,1,0:T(8,128)}) %reduce-scatter.5.cloned.1.call-update) | async-done | bytes 524304 | tf_op jit(solution)/shard_map/reduce_scatter | solution.py:52
  (24 shorter events, 3.5 us)
Async XLA Ops:
  7.2 190.0 %copy-start = (f32[64,512]{1,0:T(8,128)S(1)}, f32[64,512]{1,0:T(8,128)}, u32[]{:S(2)}) copy-start(f32[64,512]{1,0:T(8,128)} %param.7) | copy-start | bytes 393220
  7.2 190.0 %reduce-scatter.3.cloned.1.call-start = ((), (), s32[]{:S(2)}) async-start(), calls=%async_computation.2 | async-start | bytes 2621440 | tf_op jit(solution)/shard_map/reduce_scatter | solution.py:51
  8.2 12.0 %collective-permute-start.1 = (f32[1,64,512]{2,1,0:T(8,128)S(1)}, f32[1,64,512]{2,1,0:T(8,128)S(1)}, u32[]{:S(2)}, u32[]{:S(2)}) collective-permute-start(f32[1,64,512]{2,1,0:T(8,128)S(1)} %get-tuple-element.18), channel_id=1, source_target_pairs={{0,4},{4,8},{8,12},{12,16},{16,20},{20,24},{24,28},{1,5},{5,9},{9,... | collective-permute-start | bytes 393224 | tf_op jit(solution)/shard_map/ppermute | solution.py:17
  10.7 9.7 %collective-permute-start = (f32[1,64,512]{2,1,0:T(8,128)S(1)}, f32[1,64,512]{2,1,0:T(8,128)S(1)}, u32[]{:S(2)}, u32[]{:S(2)}) collective-permute-start(f32[1,64,512]{2,1,0:T(8,128)S(1)} %get-tuple-element.19), channel_id=1, source_target_pairs={{4,0},{8,4},{12,8},{16,12},{20,16},{24,20},{28,24},{5,1},{9,5},{13... | collective-permute-start | bytes 393224 | tf_op jit(solution)/shard_map/ppermute | solution.py:18
  20.2 3.4 %copy-start.1 = (f32[64,64,512]{2,0,1:T(8,128)}, f32[64,64,512]{2,0,1:T(8,128)S(1)}, u32[]{:S(2)}) copy-start(f32[64,64,512]{2,0,1:T(8,128)S(1)} %copy.43) | copy-start | bytes 25165828
  23.6 7.4 %collective-permute-start.2 = (f32[66,1,512]{2,0,1:T(8,128)S(1)}, f32[66,1,512]{2,0,1:T(8,128)S(1)}, u32[]{:S(2)}, u32[]{:S(2)}) collective-permute-start(f32[66,1,512]{2,0,1:T(8,128)S(1)} %get-tuple-element.14), channel_id=1, source_target_pairs={{1,0},{2,1},{3,2},{5,4},{6,5},{7,6},{9,8},{10,9},{11,10},{13,12},{... | collective-permute-start | bytes 405512 | tf_op jit(solution)/shard_map/ppermute | solution.py:18
  24.9 7.6 %collective-permute-start.3 = (f32[66,1,512]{2,0,1:T(8,128)S(1)}, f32[66,1,512]{2,0,1:T(8,128)S(1)}, u32[]{:S(2)}, u32[]{:S(2)}) collective-permute-start(f32[66,1,512]{2,0,1:T(8,128)S(1)} %get-tuple-element.15), channel_id=1, source_target_pairs={{0,1},{1,2},{2,3},{4,5},{5,6},{6,7},{8,9},{9,10},{10,11},{12,13},{... | collective-permute-start | bytes 405512 | tf_op jit(solution)/shard_map/ppermute | solution.py:17
  76.6 5.6 %collective-permute-start.4 = (f32[1,64,512]{2,1,0:T(8,128)S(1)}, f32[1,64,512]{2,1,0:T(8,128)S(1)}, u32[]{:S(2)}, u32[]{:S(2)}) collective-permute-start(f32[1,64,512]{2,1,0:T(8,128)S(1)} %copy.36), channel_id=1, source_target_pairs={{4,0},{8,4},{12,8},{16,12},{20,16},{24,20},{28,24},{5,1},{9,5},{13... | collective-permute-start | bytes 393224 | tf_op jit(solution)/shard_map/ppermute | solution.py:18
  77.9 5.2 %collective-permute-start.5 = (f32[1,64,512]{2,1,0:T(8,128)S(1)}, f32[1,64,512]{2,1,0:T(8,128)S(1)}, u32[]{:S(2)}, u32[]{:S(2)}) collective-permute-start(f32[1,64,512]{2,1,0:T(8,128)S(1)} %copy.38), channel_id=1, source_target_pairs={{0,4},{4,8},{8,12},{12,16},{16,20},{20,24},{24,28},{1,5},{5,9},{9,... | collective-permute-start | bytes 393224 | tf_op jit(solution)/shard_map/ppermute | solution.py:17
  84.2 7.2 %collective-permute-start.6 = (f32[66,1,512]{2,0,1:T(8,128)S(1)}, f32[66,1,512]{2,0,1:T(8,128)S(1)}, u32[]{:S(2)}, u32[]{:S(2)}) collective-permute-start(f32[66,1,512]{2,0,1:T(8,128)S(1)} %get-tuple-element.12), channel_id=1, source_target_pairs={{1,0},{2,1},{3,2},{5,4},{6,5},{7,6},{9,8},{10,9},{11,10},{13,12},{... | collective-permute-start | bytes 405512 | tf_op jit(solution)/shard_map/ppermute | solution.py:18
  85.5 7.4 %collective-permute-start.7 = (f32[66,1,512]{2,0,1:T(8,128)S(1)}, f32[66,1,512]{2,0,1:T(8,128)S(1)}, u32[]{:S(2)}, u32[]{:S(2)}) collective-permute-start(f32[66,1,512]{2,0,1:T(8,128)S(1)} %get-tuple-element.13), channel_id=1, source_target_pairs={{0,1},{1,2},{2,3},{4,5},{5,6},{6,7},{8,9},{9,10},{10,11},{12,13},{... | collective-permute-start | bytes 405512 | tf_op jit(solution)/shard_map/ppermute | solution.py:17
  92.9 44.1 %copy-start.3 = (bf16[512,128]{1,0:T(8,128)(2,1)S(1)}, bf16[512,128]{1,0:T(8,128)(2,1)}, u32[]{:S(2)}) copy-start(bf16[512,128]{1,0:T(8,128)(2,1)} %param.9) | copy-start | bytes 393220
  92.9 48.7 %copy-start.2 = (f32[64,64]{1,0:T(8,128)S(1)}, f32[64,64]{1,0:T(8,128)}, u32[]{:S(2)}) copy-start(f32[64,64]{1,0:T(8,128)} %param.8) | copy-start | bytes 49156
  145.0 114.2 %reduce-scatter.5.cloned.1.call-start = ((), (), s32[]{:S(2)}) async-start(), calls=%async_computation.3 | async-start | bytes 4718592 | tf_op jit(solution)/shard_map/reduce_scatter | solution.py:52
Sparse Core Ops, SparseCore 0:
  145.1 52.0 reduce-scatter.2
  208.8 50.3 reduce-scatter.4
where the time goes:
time: 267 us; the launch traced here: 266 us
  waiting for transfers between devices  96.5 us (36%)
  other arithmetic  87.3 us (33%)
  local copies, waits for them, and re-layouts  32.1 us (12%)
  starting transfers between devices  21.9 us (8%)
  between operations  14.2 us (5%)
  matrix products  14.1 us (5%)
    reduce_scatter x1, waiting for transfers between devices, on_device(): y_owned = lax.psum_scatter(y_reduced, 'gy', scatter_dimension=1, tiled=True)  52.1 us
    convert_element_type x1, other arithmetic, on_device(): lowered = advanced.astype(jnp.bfloat16)  44.1 us
    add x1, other arithmetic, on_device(): middle = scalar + first  42.2 us
    reduce_scatter x1, waiting for transfers between devices, on_device(): lax.psum_scatter(jnp.einsum('xa,xbc->abc', factor_x, y_owned, precision=l...  38.6 us
    unnamed x10, local copies, waits for them, and re-layouts  23.2 us
    ppermute x4, starting transfers between devices, extended(): before = lax.ppermute(last, axis, up)  16.7 us
    dot_general x1, matrix products, on_device(): jnp.einsum('xa,xbc->abc', factor_x, y_owned, precision=lax.Precision.HIGH...  6.06 us
    dot_general x1, local copies, waits for them, and re-layouts, on_device(): jnp.einsum('xa,xbc->abc', factor_x, y_owned, precision=lax.Precision.HIGH...  5.45 us
  transfers between devices with their start and end apart: 10, of which 7 were waited for; matrix products, arithmetic and copies ran while one was open for 8% of the time, Pallas kernels for 0%

commit v1 on v0

v1 whole, which is shorter than its diff:
```python
import functools
import math

import jax
import jax.numpy as jnp
from jax import lax
from jax.experimental import pallas as pl
from jax.experimental.pallas import tpu as pltpu
from jax.sharding import PartitionSpec as P

spread_rate = 0.12
activation = 2.0
exponent = -activation * math.log2(math.e)
lanes = 128
pad = 8
chunks = 4
f32, bf16 = jnp.float32, jnp.bfloat16
anywhere = pl.BlockSpec(memory_space=pltpu.HBM)
in_vmem = pl.BlockSpec(memory_space=pltpu.VMEM)


def source(field, prefactor):
    return prefactor * jnp.exp2(exponent / (1.0 + field * field))


def along_z(tiles):
    lane = lax.broadcasted_iota(jnp.int32, tiles[0].shape, 1)
    last = len(tiles) - 1
    sums = []
    for k, tile in enumerate(tiles):
        below = tiles[k - 1] if k else 0.0
        above = tiles[k + 1] if k < last else 0.0
        left = pltpu.roll(jnp.where(lane == lanes - 1, below, tile), 1, 1)
        right = pltpu.roll(jnp.where(lane == 0, above, tile), lanes - 1, 1)
        sums.append(left + right)
    return sums


def column(k):
    return slice(k * lanes, (k + 1) * lanes)


def faces_kernel(scalar, prefactor, x_lo, x_hi, y_lo, y_hi, s_rows, p_rows, s_cols, p_cols, line, sems):
    cells_x, cells_y, depth = scalar.shape
    copies = [
        (scalar.at[pl.ds(0, 2)], s_rows.at[0]),
        (scalar.at[pl.ds(cells_x - 2, 2)], s_rows.at[1]),
        (prefactor.at[pl.ds(0, 1)], p_rows.at[0]),
        (prefactor.at[pl.ds(cells_x - 1, 1)], p_rows.at[1]),
        (scalar.at[:, pl.ds(0, 8)], s_cols.at[0]),
        (prefactor.at[:, pl.ds(0, 8)], p_cols.at[0]),
        (scalar.at[:, pl.ds(cells_y - 8, 8)], s_cols.at[1]),
        (prefactor.at[:, pl.ds(cells_y - 8, 8)], p_cols.at[1]),
    ]
    copies = [pltpu.make_async_copy(a, b, sems.at[n]) for n, (a, b) in enumerate(copies)]
    for copy in copies:
        copy.start()
    tiles = depth // lanes

    def face(out, outer, inner, factor, count, tiled=False):
        line[:, 0:pad, :] = jnp.zeros((tiles, pad, lanes), f32)
        line[:, pad + count : 2 * pad + count, :] = jnp.zeros((tiles, pad, lanes), f32)
        own = [outer(k) for k in range(tiles)]
        for k in range(tiles):
            line[k, pad : pad + count, :] = own[k]
        for k, z_sum in enumerate(along_z(own)):
            beside = line[k, pad - 1 : pad - 1 + count, :] + line[k, pad + 1 : pad + 1 + count, :]
            beside = beside + z_sum + inner(k)
            at = (k, slice(None), slice(None)) if tiled else (slice(None), column(k))
            out[(0,) + at] = own[k]
            out[(1,) + at] = (
                spread_rate * beside + (1.0 - 6.0 * spread_rate) * own[k] + source(own[k], factor(k))
            )

    for n in range(4):
        copies[n].wait()
    face(x_lo, lambda k: s_rows[0, 0, :, column(k)], lambda k: s_rows[0, 1, :, column(k)],
         lambda k: p_rows[0, 0, :, column(k)], cells_y)
    face(x_hi, lambda k: s_rows[1, 1, :, column(k)], lambda k: s_rows[1, 0, :, column(k)],
         lambda k: p_rows[1, 0, :, column(k)], cells_y)
    for n in range(4, 8):
        copies[n].wait()
    face(y_lo, lambda k: s_cols[0, :, 0, column(k)], lambda k: s_cols[0, :, 1, column(k)],
         lambda k: p_cols[0, :, 0, column(k)], cells_x, True)
    face(y_hi, lambda k: s_cols[1, :, 7, column(k)], lambda k: s_cols[1, :, 6, column(k)],
         lambda k: p_cols[1, :, 7, column(k)], cells_x, True)


def faces(scalar, prefactor):
    cells_x, cells_y, depth = scalar.shape
    x_face = jax.ShapeDtypeStruct((2, cells_y, depth), f32)
    y_face = jax.ShapeDtypeStruct((2, depth // lanes, cells_x, lanes), f32)
    longest = max(cells_x, cells_y)
    return pl.pallas_call(
        faces_kernel,
        out_shape=(x_face, x_face, y_face, y_face),
        in_specs=[anywhere, anywhere],
        out_specs=[in_vmem] * 4,
        scratch_shapes=[
            pltpu.VMEM((2, 2, cells_y, depth), f32),
            pltpu.VMEM((2, 1, cells_y, depth), f32),
            pltpu.VMEM((2, cells_x, 8, depth), f32),
            pltpu.VMEM((2, cells_x, 8, depth), f32),
            pltpu.VMEM((depth // lanes, longest + 2 * pad, lanes), f32),
            pltpu.SemaphoreType.DMA((8,)),
        ],
        name="faces",
    )(scalar, prefactor)


def rows_kernel(
    first_row, rows, flags, scalar, prefactor, x_lo, x_hi, y_lo, y_hi, c_lo, c_hi, factor_z, mix, *rest
):
    (advanced, keep, send, s_buf, p_buf, m_buf, a_buf, low_buf, z_buf, e_buf, s_sem, p_sem, a_sem, e_sem) = rest[-14:]
    cells_x, cells_y, depth = scalar.shape
    tiles = depth // lanes
    inner = pl.ds(pad, cells_y)
    at_lo, at_hi = first_row == 0, first_row + rows == cells_x
    first_slot, end_slot = (2 if at_lo else 0), (rows + 2 if at_hi else rows + 4)
    first_m, end_m = (1 if at_lo else 0), (rows + 1 if at_hi else rows + 2)

    def s_copy(slot, k):
        return pltpu.make_async_copy(
            scalar.at[first_row - 2 + slot, :, pl.ds(k * lanes, lanes)], s_buf.at[k, slot, inner], s_sem.at[slot, k]
        )

    def p_copy(slot):
        return pltpu.make_async_copy(prefactor.at[first_row - 1 + slot], p_buf.at[slot], p_sem.at[slot])

    def a_copy(row):
        return pltpu.make_async_copy(a_buf.at[row], advanced.at[first_row + row], a_sem.at[row])

    def edge_copies(face, slot, n):
        return [
            pltpu.make_async_copy(
                face.at[0, :, pl.ds(k * lanes, lanes)], s_buf.at[k, slot, inner], s_sem.at[slot, k]
            )
            for k in range(tiles)
        ] + [pltpu.make_async_copy(face.at[1], e_buf.at[n], e_sem.at[n])]

    def start(slot, carry):
        for k in range(tiles):
            s_copy(slot, k).start()

        @pl.when(jnp.logical_and(slot - 1 >= first_m, slot - 1 < end_m))
        def _():
            p_copy(slot - 1).start()

        return carry

    if at_lo:
        for copy in edge_copies(x_lo, 1, 0):
            copy.start()
    lax.fori_loop(first_slot, end_slot, start, 0)
    if at_hi:
        for copy in edge_copies(x_hi, rows + 2, 1):
            copy.start()

    def y_rows(slot):
        row = first_row - 2 + slot
        for k in range(tiles):
            s_buf[k, slot, pad - 1 : pad, :] = y_lo[0, k, pl.ds(row, 1), :]
            s_buf[k, slot, pad + cells_y : pad + cells_y + 1, :] = y_hi[0, k, pl.ds(row, 1), :]

    def neighbours(buf, slot):
        own = [buf[k, slot, inner, :] for k in range(tiles)]
        sums = []
        for k, z_sum in enumerate(along_z(own)):
            beside = buf[k, slot - 1, inner, :] + buf[k, slot + 1, inner, :]
            beside = beside + (buf[k, slot, pl.ds(pad - 1, cells_y), :] + buf[k, slot, pl.ds(pad + 1, cells_y), :])
            sums.append(beside + z_sum)
        return own, sums

    def stage_one(slot):
        y_rows(slot + 1)
        own, sums = neighbours(s_buf, slot + 1)
        for k in range(tiles):
            middle = spread_rate * sums[k] + (
                (1.0 - 6.0 * spread_rate) * own[k] + source(own[k], p_buf[slot, :, column(k)])
            )
            m_buf[k, slot, inner, :] = middle

    def m_rows(slot):
        row = first_row - 1 + slot
        for k in range(tiles):
            m_buf[k, slot, pad - 1 : pad, :] = (
                y_lo[1, k, pl.ds(row, 1), :] + flags[2] * s_buf[k, slot + 1, pad : pad + 1, :]
            )
            m_buf[k, slot, pad + cells_y : pad + cells_y + 1, :] = (
                y_hi[1, k, pl.ds(row, 1), :]
                + flags[3] * s_buf[k, slot + 1, pad + cells_y - 1 : pad + cells_y, :]
            )

    def stage_two(row):
        slot = row + 1
        own, sums = neighbours(m_buf, slot)
        for k in range(tiles):
            value = source(own[k], p_buf[slot, :, column(k)]) + s_buf[k, slot + 1, inner, :]
            value = 0.5 * (value + (spread_rate * sums[k] + (1.0 - 6.0 * spread_rate) * own[k]))
            a_buf[row, :, column(k)] = value
            low_buf[row, :, column(k)] = value.astype(bf16)

    def wait_s(slot):
        for k in range(tiles):
            s_copy(slot, k).wait()

    def corner(buf_row, slot, index):
        for k in range(tiles):
            m_buf[k, slot, pad : pad + 1, :] += spread_rate * c_lo[index : index + 1, column(k)]
            end = pad + cells_y
            m_buf[k, slot, end - 1 : end, :] += spread_rate * c_hi[index : index + 1, column(k)]

    def edge(n, slot, beside, index):
        for k in range(tiles):
            m_buf[k, slot, inner, :] = e_buf[n, :, column(k)] + flags[n] * s_buf[k, beside, inner, :]
        corner(None, slot, index)

    def ends(slot, index):
        for k in range(tiles):
            m_buf[k, slot, pad - 1 : pad, :] += spread_rate * c_lo[index : index + 1, column(k)]
            end = pad + cells_y
            m_buf[k, slot, end : end + 1, :] += spread_rate * c_hi[index : index + 1, column(k)]

    if at_lo:
        for copy in edge_copies(x_lo, 1, 0):
            copy.wait()
        wait_s(2)
        wait_s(3)
        p_copy(1).wait()
        edge(0, 0, 2, 0)
        stage_one(1)
        m_rows(1)
        ends(1, 0)
    else:
        for slot in range(4):
            wait_s(slot)
        for slot in range(2):
            p_copy(slot).wait()
            stage_one(slot)
        m_rows(1)

    def step(t, carry):
        wait_s(t + 2)
        p_copy(t).wait()
        stage_one(t)
        m_rows(t)
        stage_two(t - 2)
        a_copy(t - 2).start()
        return carry

    if at_hi:
        lax.fori_loop(2, rows, step, 0)
        for copy in edge_copies(x_hi, rows + 2, 1):
            copy.wait()
        p_copy(rows).wait()
        stage_one(rows)
        m_rows(rows)
        ends(rows, 1)
        stage_two(rows - 2)
        a_copy(rows - 2).start()
        edge(1, rows + 1, rows + 1, 1)
    else:
        lax.fori_loop(2, rows + 1, step, 0)
        wait_s(rows + 3)
        p_copy(rows + 1).wait()
        stage_one(rows + 1)
    stage_two(rows - 1)
    a_copy(rows - 1).start()

    half = keep.shape[1]
    for row in range(rows):
        z_buf[row] = jnp.dot(low_buf[row], factor_z[...], preferred_element_type=f32)
    for row in range(rows):
        z = z_buf[row]
        high = z.astype(bf16)
        low = (z - high.astype(f32)).astype(bf16)
        y = jnp.dot(mix[...], jnp.concatenate([high, low, high], axis=0), preferred_element_type=f32)
        keep[row] = y[:half]
        send[row] = y[half:]

    def finish(row, carry):
        a_copy(row).wait()
        return carry

    lax.fori_loop(0, rows, finish, 0)


def run_of_rows(index, rows, flags, scalar, prefactor, halos, factor_z, mix, previous):
    cells_x, cells_y, depth = scalar.shape
    ranks = mix.shape[0]
    z_rank = factor_z.shape[1]
    tiles = depth // lanes
    part = jax.ShapeDtypeStruct((rows, ranks // 2, z_rank), f32)
    x_lo, x_hi, y_lo, y_hi, c_lo, c_hi = halos
    operands = [flags, scalar, prefactor, x_lo, x_hi, y_lo, y_hi, c_lo, c_hi, factor_z, mix]
    specs = [pl.BlockSpec(memory_space=pltpu.SMEM)] + [anywhere] * 4 + [in_vmem] * 6
    aliases = {}
    if previous is not None:
        operands.append(previous)
        specs.append(anywhere)
        aliases = {len(operands) - 1: 0}
    plane = (cells_y + 2 * pad, lanes)
    cells = rows * cells_y * depth
    return pl.pallas_call(
        functools.partial(rows_kernel, index * rows, rows),
        out_shape=(jax.ShapeDtypeStruct(scalar.shape, f32), part, part),
        in_specs=specs,
        out_specs=[anywhere, in_vmem, in_vmem],
        input_output_aliases=aliases,
        scratch_shapes=[
            pltpu.VMEM((tiles, rows + 4) + plane, f32),
            pltpu.VMEM((rows + 2, cells_y, depth), f32),
            pltpu.VMEM((tiles, rows + 2) + plane, f32),
            pltpu.VMEM((rows, cells_y, depth), f32),
            pltpu.VMEM((rows, cells_y, depth), bf16),
            pltpu.VMEM((rows, cells_y, z_rank), f32),
            pltpu.VMEM((2, cells_y, depth), f32),
            pltpu.SemaphoreType.DMA((rows + 4, tiles)),
            pltpu.SemaphoreType.DMA((rows + 2,)),
            pltpu.SemaphoreType.DMA((rows,)),
            pltpu.SemaphoreType.DMA((2,)),
        ],
        cost_estimate=pl.CostEstimate(
            flops=60 * cells + 2 * cells * z_rank, bytes_accessed=12 * cells, transcendentals=4 * cells
        ),
        name=f"rows_{index}",
    )(*operands)


def shift(array, axis, step):
    peers = lax.axis_size(axis)
    return lax.ppermute(array, axis, [(i, i + step) for i in range(peers) if 0 <= i + step < peers])


def swap(array, axis, distance):
    return lax.ppermute(array, axis, [(i, i ^ distance) for i in range(lax.axis_size(axis))])


def gathered(array, axis):
    peers, distance = lax.axis_size(axis), 1
    me = lax.axis_index(axis)
    while distance < peers:
        other = swap(array, axis, distance)
        upper = (me & distance) != 0
        array = jnp.concatenate([jnp.where(upper, other, array), jnp.where(upper, array, other)], axis=0)
        distance *= 2
    return array


def split(array):
    high = lax.reduce_precision(array, 8, 7)
    return high.astype(bf16), (array - high).astype(bf16)


def on_device(scalar, prefactor, factor_x, factor_y, factor_z):
    cells_x, cells_y, depth = scalar.shape
    peers_x, peers_y = lax.axis_size("gx"), lax.axis_size("gy")
    at_x, at_y = lax.axis_index("gx"), lax.axis_index("gy")
    y_rank, z_rank = factor_y.shape[1], factor_z.shape[1]
    block = y_rank // peers_y

    x_lo, x_hi, y_lo, y_hi = faces(scalar, prefactor)
    from_x_lo, from_x_hi = shift(x_hi, "gx", 1), shift(x_lo, "gx", -1)
    from_y_lo, from_y_hi = shift(y_hi, "gy", 1), shift(y_lo, "gy", -1)
    beside = jnp.stack([from_x_lo[0], from_x_hi[0]])
    c_lo = shift(beside[:, cells_y - 1], "gy", 1)
    c_hi = shift(beside[:, 0], "gy", -1)
    halos = (from_x_lo, from_x_hi, from_y_lo, from_y_hi, c_lo, c_hi)
    flags = spread_rate * jnp.stack(
        [at_x > 0, at_x < peers_x - 1, at_y > 0, at_y < peers_y - 1]
    ).astype(f32)

    bits = peers_y.bit_length() - 1
    order = jnp.array([int(format(n, f"0{bits}b")[::-1], 2) if bits else 0 for n in range(peers_y)])
    blocks = factor_y.T.reshape(peers_y, block, cells_y)
    ordered = jnp.take(blocks, order ^ at_y, axis=0).reshape(y_rank, cells_y)
    high, low = split(ordered)
    mix = jnp.concatenate([high, high, low], axis=1)

    all_x = gathered(factor_x, "gx")

    rows = cells_x // chunks
    advanced, owned = None, []
    for index in range(chunks):
        advanced, keep, send = run_of_rows(
            index, rows, flags, scalar, prefactor, halos, factor_z, mix, advanced
        )
        distance = 1
        while True:
            keep = keep + swap(send, "gy", distance)
            distance *= 2
            if distance == peers_y:
                break
            half = keep.shape[1] // 2
            keep, send = keep[:, :half], keep[:, half:]
        owned.append(keep)
    owned = jnp.concatenate(owned, axis=0)

    columns = block * z_rank // peers_x
    parts = owned.reshape(cells_x, peers_x, columns).transpose(1, 0, 2)
    parts = lax.all_to_all(parts, "gx", 0, 0, tiled=True).reshape(peers_x * cells_x, columns)
    core = jnp.einsum("xa,xn->an", all_x, parts, precision=lax.Precision.HIGHEST)
    core = core.reshape(peers_x, -1, columns)
    core = lax.all_to_all(core, "gx", 0, 0, tiled=True)
    core = core.transpose(1, 0, 2).reshape(-1, block, z_rank)
    return (advanced, core)


def solution(mesh):
    return jax.shard_map(
        on_device,
        mesh=mesh,
        in_specs=(P("gx", "gy", None), P("gx", "gy", None), P("gx", None), P("gy", None), P()),
        out_specs=(P("gx", "gy", None), P("gx", "gy", None)),
        check_vma=False,
    )
```

time: 267 us -> 128 us (0.48)
  other arithmetic: 87.3 us -> 2.91 us
  waiting for transfers between devices: 96.5 us -> 28.7 us
  Pallas kernels: 0 us -> 39.1 us
  local copies, waits for them, and re-layouts: 32.1 us -> 8.02 us
  between operations: 14.2 us -> 1.07 us
  matrix products: 14.1 us -> 0.98 us
  starting transfers between devices: 21.9 us -> 34.5 us
  blocking collectives: 0 us -> 12.1 us
    reduce_scatter x2 -> x0, waiting for transfers between devices: 90.8 us -> none  [the longest x1 52.1 us: on_device(): y_owned = lax.psum_scatter(y_reduced, 'gy', scatter_dimension=1, tiled=True)]
    convert_element_type x1, other arithmetic: 44.1 us -> 0.08 us  [split(): return (high.astype(bf16), (array - high).astype(bf16))]
    add x1 -> x8, other arithmetic: 42.2 us -> 1.17 us  [on_device(): keep = keep + swap(send, 'gy', distance)]
    pallas_call x0 -> x5, Pallas kernels: none -> 39.1 us  [the longest x4 34.8 us: run_of_rows(): pl.pallas_call(functools.partial(rows_kernel, index * rows, rows), out_sh...]
    unnamed x10 -> x21, local copies, waits for them, and re-layouts: 23.2 us -> 0.7 us
    ppermute x8 -> x17, waiting for transfers between devices: 5.71 us -> 19.6 us  [the longest x11 17 us: swap(): lax.ppermute(array, axis, [(i, i ^ distance) for i in range(lax.axis_size...]
    dot_general x3 -> x1, matrix products: 14.1 us -> 0.98 us  [on_device(): jnp.einsum('xa,xn->an', all_x, parts, precision=lax.Precision.HIGHEST)]
    all_to_all x0 -> x1, blocking collectives: none -> 12.1 us  [on_device(): core = lax.all_to_all(core, 'gx', 0, 0, tiled=True)]
  transfers between devices with their start and end apart: 10 -> 18, of which waited for: 7 -> 6; matrix products, arithmetic and copies ran while one was open for 8% -> 6% of each run, Pallas kernels for 0% -> 21%
where the time goes in v1:
time: 128 us; the launch traced here: 127 us
  Pallas kernels  39.1 us (31%)
  starting transfers between devices  34.5 us (27%)
  waiting for transfers between devices  28.7 us (22%)
  blocking collectives  12.1 us (9%)
  local copies, waits for them, and re-layouts  8.02 us (6%)
  other arithmetic  2.91 us (2%)
    pallas_call x4, Pallas kernels, run_of_rows(): pl.pallas_call(functools.partial(rows_kernel, index * rows, rows), out_sh...  34.8 us
    ppermute x11, waiting for transfers between devices, swap(): lax.ppermute(array, axis, [(i, i ^ distance) for i in range(lax.axis_size...  17 us
    ppermute x11, starting transfers between devices, swap(): lax.ppermute(array, axis, [(i, i ^ distance) for i in range(lax.axis_size...  16.1 us
    ppermute x6, starting transfers between devices, shift(): lax.ppermute(array, axis, [(i, i + step) for i in range(peers) if 0 <= i...  14.9 us
    all_to_all x1, blocking collectives, on_device(): core = lax.all_to_all(core, 'gx', 0, 0, tiled=True)  12.1 us
    all_to_all x1, waiting for transfers between devices, on_device(): lax.all_to_all(parts, 'gx', 0, 0, tiled=True)  9.09 us
    pallas_call x1, Pallas kernels, faces(): pl.pallas_call(faces_kernel, out_shape=(x_face, x_face, y_face, y_face),...  4.28 us
    all_to_all x1, starting transfers between devices, on_device(): lax.all_to_all(parts, 'gx', 0, 0, tiled=True)  3.49 us
  transfers between devices with their start and end apart: 18, of which 6 were waited for; matrix products, arithmetic and copies ran while one was open for 6% of the time, Pallas kernels for 21%

profile of v1, /device:TPU:0, one launch (start us, length us, event | category | flops | bytes accessed | tf_op | source)
XLA Modules:
  0.0 127.4 jit_solution(14826376475684449458)
XLA Ops:
  0.7 4.3 %faces.1 = (f32[2,64,512]{2,1,0:T(8,128)}, f32[2,64,512]{2,1,0:T(8,128)}, f32[2,4,64,128]{3,2,1,0:T(8,128)}, f32[2,4,64,128]{3,2,1,0:T(8,128)}) custom-call(f32[64,64,512]{2,1,0:T(8,128)} %scalar.9, f32[64,64,512]{2,1,0:T(8,128)} %prefactor.9), custom_call_target="tpu_custom_call" | custom-call | tf_op jit(solution)/shard_map/faces/pallas_call | solution.py:94
  6.1 2.4 %collective-permute-start = (f32[2,64,512]{2,0,1:T(2,128)S(1)}, f32[2,64,512]{2,0,1:T(2,128)S(1)}, u32[]{:S(2)}, u32[]{:S(2)}) collective-permute-start(f32[2,64,512]{2,0,1:T(2,128)S(1)} %copy.37), channel_id=1, source_target_pairs={{0,4},{4,8},{8,12},{12,16},{16,20},{20,24},{24,28},{1,5},{5,9},{9,... | collective-permute-start | bytes 786440 | tf_op jit(solution)/shard_map/ppermute | solution.py:332
  11.0 4.3 %collective-permute-start.2 = (f32[2,4,64,128]{3,2,1,0:T(8,128)}, f32[2,4,64,128]{3,2,1,0:T(8,128)S(1)}, u32[]{:S(2)}, u32[]{:S(2)}) collective-permute-start(f32[2,4,64,128]{3,2,1,0:T(8,128)} %get-tuple-element.20), channel_id=1, source_target_pairs={{0,1},{1,2},{2,3},{4,5},{5,6},{6,7},{8,9},{9,10},{10,11},{12,13},{... | collective-permute-start | bytes 786440 | tf_op jit(solution)/shard_map/ppermute | solution.py:332
  16.6 2.2 %collective-permute-start.6 = (f32[64,512]{1,0:T(8,128)S(1)}, f32[64,512]{1,0:T(8,128)S(1)}, u32[]{:S(2)}, u32[]{:S(2)}) collective-permute-start(f32[64,512]{1,0:T(8,128)S(1)} %copy-done.5), channel_id=1, source_target_pairs={{0,4},{4,0},{8,12},{12,8},{16,20},{20,16},{24,28},{28,24},{1,5},{5... | collective-permute-start | bytes 393224 | tf_op jit(solution)/shard_map/ppermute | solution.py:336
  21.3 4.3 %collective-permute-start.4 = (f32[2,512]{1,0:T(2,128)S(1)}, f32[2,512]{1,0:T(2,128)S(1)}, u32[]{:S(2)}, u32[]{:S(2)}) collective-permute-start(f32[2,512]{1,0:T(2,128)S(1)} %get-tuple-element.43), channel_id=1, source_target_pairs={{0,1},{1,2},{2,3},{4,5},{5,6},{6,7},{8,9},{9,10},{10,11},{12,13},{... | collective-permute-start | bytes 12296 | tf_op jit(solution)/shard_map/ppermute | solution.py:332
  25.5 1.3 %collective-permute-start.5 = (f32[2,512]{1,0:T(2,128)S(1)}, f32[2,512]{1,0:T(2,128)S(1)}, u32[]{:S(2)}, u32[]{:S(2)}) collective-permute-start(f32[2,512]{1,0:T(2,128)S(1)} %get-tuple-element.42), channel_id=1, source_target_pairs={{1,0},{2,1},{3,2},{5,4},{6,5},{7,6},{9,8},{10,9},{11,10},{13,12},{... | collective-permute-start | bytes 12296 | tf_op jit(solution)/shard_map/ppermute | solution.py:332
  28.4 2.6 %collective-permute-done.5.c_hi = f32[2,512]{1,0:T(2,128)S(1)} collective-permute-done((f32[2,512]{1,0:T(2,128)S(1)}, f32[2,512]{1,0:T(2,128)S(1)}, u32[]{:S(2)}, u32[]{:S(2)}) %collective-permute-start.5) | collective-permute-done | bytes 4128 | tf_op jit(solution)/shard_map/ppermute | solution.py:332
  31.6 8.6 %rows_0.1 = (f32[64,64,512]{2,1,0:T(8,128)}, f32[16,32,128]{2,1,0:T(8,128)}, f32[16,32,128]{2,1,0:T(8,128)}) custom-call(f32[4]{0:T(128)} %add_select_fusion.flags, f32[64,64,512]{2,1,0:T(8,128)} %scalar.9, f32[64,64,512]{2,1,0:T(8,128)} %prefactor.9, f32[2,64,512]{2,1,0:T(8,128)} %copy.46.x_lo, f32[2,64,512]{2,1,0:T(8,128)} %copy.47.x_hi, ...), custom_call_target="tpu_custom_call" | custom-call | flops 165675008 | bytes 6291456 | tf_op jit(solution)/shard_map/rows_0/pallas_call | solution.py:304
  40.3 1.6 %collective-permute-start.9 = (f32[16,32,128]{2,1,0:T(8,128)}, f32[16,32,128]{2,1,0:T(8,128)S(1)}, u32[]{:S(2)}, u32[]{:S(2)}) collective-permute-start(f32[16,32,128]{2,1,0:T(8,128)} %get-tuple-element.27), channel_id=1, source_target_pairs={{0,1},{1,0},{2,3},{3,2},{4,5},{5,4},{6,7},{7,6},{8,9},{9,8},{10,11... | collective-permute-start | bytes 786440 | tf_op jit(solution)/shard_map/ppermute | solution.py:336
  41.9 2.3 %collective-permute-start.7 = (f32[128,512]{1,0:T(8,128)S(1)}, f32[128,512]{1,0:T(8,128)S(1)}, u32[]{:S(2)}, u32[]{:S(2)}) collective-permute-start(f32[128,512]{1,0:T(8,128)S(1)} %pad_maximum_fusion.2), channel_id=1, source_target_pairs={{0,8},{4,12},{8,0},{12,4},{16,24},{20,28},{24,16},{28,20},{1,9},{5... | collective-permute-start | bytes 786440 | tf_op jit(solution)/shard_map/ppermute | solution.py:336
  44.2 8.7 %rows_1.1 = (f32[64,64,512]{2,1,0:T(8,128)}, f32[16,32,128]{2,1,0:T(8,128)}, f32[16,32,128]{2,1,0:T(8,128)}) custom-call(f32[4]{0:T(128)} %add_select_fusion.flags, f32[64,64,512]{2,1,0:T(8,128)} %scalar.9, f32[64,64,512]{2,1,0:T(8,128)} %prefactor.9, f32[2,64,512]{2,1,0:T(8,128)} %copy.46.x_lo, ...), custom_call_target="tpu_custom_call", output_to_operand_aliasing={{0}: (11, {})} | custom-call | flops 165675008 | bytes 6291456 | tf_op jit(solution)/shard_map/rows_1/pallas_call | solution.py:304
  53.5 8.7 %rows_2.1 = (f32[64,64,512]{2,1,0:T(8,128)}, f32[16,32,128]{2,1,0:T(8,128)}, f32[16,32,128]{2,1,0:T(8,128)}) custom-call(f32[4]{0:T(128)} %add_select_fusion.flags, f32[64,64,512]{2,1,0:T(8,128)} %scalar.9, f32[64,64,512]{2,1,0:T(8,128)} %prefactor.9, f32[2,64,512]{2,1,0:T(8,128)} %copy.46.x_lo, ...), custom_call_target="tpu_custom_call", output_to_operand_aliasing={{0}: (11, {})} | custom-call | flops 165675008 | bytes 6291456 | tf_op jit(solution)/shard_map/rows_2/pallas_call | solution.py:304
  62.2 1.6 %collective-permute-start.13 = (f32[16,32,128]{2,1,0:T(8,128)}, f32[16,32,128]{2,1,0:T(8,128)S(1)}, u32[]{:S(2)}, u32[]{:S(2)}) collective-permute-start(f32[16,32,128]{2,1,0:T(8,128)} %get-tuple-element.31), channel_id=1, source_target_pairs={{0,1},{1,0},{2,3},{3,2},{4,5},{5,4},{6,7},{7,6},{8,9},{9,8},{10,11... | collective-permute-start | bytes 786440 | tf_op jit(solution)/shard_map/ppermute | solution.py:336
  63.8 8.7 %rows_3.1 = (f32[64,64,512]{2,1,0:T(8,128)}, f32[16,32,128]{2,1,0:T(8,128)}, f32[16,32,128]{2,1,0:T(8,128)}) custom-call(f32[4]{0:T(128)} %add_select_fusion.flags, f32[64,64,512]{2,1,0:T(8,128)} %scalar.9, f32[64,64,512]{2,1,0:T(8,128)} %prefactor.9, f32[2,64,512]{2,1,0:T(8,128)} %copy.46.x_lo, ...), custom_call_target="tpu_custom_call", output_to_operand_aliasing={{0}: (11, {})} | custom-call | flops 165675008 | bytes 6291456 | tf_op jit(solution)/shard_map/rows_3/pallas_call | solution.py:304
  73.1 2.7 %collective-permute-start.10 = (f32[16,16,128]{2,1,0:T(8,128)S(1)}, f32[16,16,128]{2,1,0:T(8,128)S(1)}, u32[]{:S(2)}, u32[]{:S(2)}) collective-permute-start(f32[16,16,128]{2,1,0:T(8,128)S(1)} %slice.53), channel_id=1, source_target_pairs={{0,2},{1,3},{2,0},{3,1},{4,6},{5,7},{6,4},{7,5},{8,10},{9,11},{10,... | collective-permute-start | bytes 393224 | tf_op jit(solution)/shard_map/ppermute | solution.py:336
  75.9 1.6 %collective-permute-start.8 = (f32[256,512]{1,0:T(8,128)S(1)}, f32[256,512]{1,0:T(8,128)S(1)}, u32[]{:S(2)}, u32[]{:S(2)}) collective-permute-start(f32[256,512]{1,0:T(8,128)S(1)} %pad_maximum_fusion), channel_id=1, source_target_pairs={{0,16},{4,20},{8,24},{12,28},{16,0},{20,4},{24,8},{28,12},{1,17},{... | collective-permute-start | bytes 1572872 | tf_op jit(solution)/shard_map/ppermute | solution.py:336
  78.0 2.7 %collective-permute-start.14 = (f32[16,16,128]{2,1,0:T(8,128)S(1)}, f32[16,16,128]{2,1,0:T(8,128)S(1)}, u32[]{:S(2)}, u32[]{:S(2)}) collective-permute-start(f32[16,16,128]{2,1,0:T(8,128)S(1)} %slice.57), channel_id=1, source_target_pairs={{0,2},{1,3},{2,0},{3,1},{4,6},{5,7},{6,4},{7,5},{8,10},{9,11},{10,... | collective-permute-start | bytes 393224 | tf_op jit(solution)/shard_map/ppermute | solution.py:336
  80.7 3.2 %collective-permute-done.15 = f32[16,32,128]{2,1,0:T(8,128)S(1)} collective-permute-done((f32[16,32,128]{2,1,0:T(8,128)}, f32[16,32,128]{2,1,0:T(8,128)S(1)}, u32[]{:S(2)}, u32[]{:S(2)}) %collective-permute-start.15) | collective-permute-done | bytes 262176 | tf_op jit(solution)/shard_map/ppermute | solution.py:336
  85.0 9.5 %collective-permute-done.12 = f32[16,16,128]{2,1,0:T(8,128)S(1)} collective-permute-done((f32[16,16,128]{2,1,0:T(8,128)S(1)}, f32[16,16,128]{2,1,0:T(8,128)S(1)}, u32[]{:S(2)}, u32[]{:S(2)}) %collective-permute-start.12) | collective-permute-done | bytes 131104 | tf_op jit(solution)/shard_map/ppermute | solution.py:336
  94.6 2.8 %collective-permute-done.14 = f32[16,16,128]{2,1,0:T(8,128)S(1)} collective-permute-done((f32[16,16,128]{2,1,0:T(8,128)S(1)}, f32[16,16,128]{2,1,0:T(8,128)S(1)}, u32[]{:S(2)}, u32[]{:S(2)}) %collective-permute-start.14) | collective-permute-done | bytes 131104 | tf_op jit(solution)/shard_map/ppermute | solution.py:336
  97.4 1.4 %collective-permute-done.16 = f32[16,16,128]{2,1,0:T(8,128)S(1)} collective-permute-done((f32[16,16,128]{2,1,0:T(8,128)S(1)}, f32[16,16,128]{2,1,0:T(8,128)S(1)}, u32[]{:S(2)}, u32[]{:S(2)}) %collective-permute-start.16) | collective-permute-done | bytes 131104 | tf_op jit(solution)/shard_map/ppermute | solution.py:336
  100.0 3.5 %all-to-all-start = ((f32[8,64,256]{2,1,0:T(8,128)}), f32[8,64,256]{2,1,0:T(8,128)S(1)}, u32[]{:S(2)}, u32[]{:S(2)}) async-start(f32[8,64,256]{2,1,0:T(8,128)} %bitcast.28), calls=%async_computation | async-start | bytes 1048576 | tf_op jit(solution)/shard_map/all_to_all | solution.py:401
  104.0 9.1 %all-to-all-done = f32[8,64,256]{2,1,0:T(8,128)S(1)} async-done(((f32[8,64,256]{2,1,0:T(8,128)}), f32[8,64,256]{2,1,0:T(8,128)S(1)}, u32[]{:S(2)}, u32[]{:S(2)}) %all-to-all-start) | async-done | bytes 524320 | tf_op jit(solution)/shard_map/all_to_all | solution.py:401
  114.1 12.1 %all_to_all.10 = f32[8,64,256]{2,1,0:T(8,128)S(1)} all-to-all(f32[8,64,256]{2,1,0:T(8,128)S(1)} %fusion.2), channel_id=1, replica_groups=mesh['gx'=8,'gy'=4] {'gx'}, dimensions={0} | all-to-all | bytes 1048576 | tf_op jit(solution)/shard_map/all_to_all | solution.py:404
  (79 shorter events, 16.0 us)
Async XLA Ops:
  0.6 18.2 %copy-start.9 = (s32[4]{0:T(128)S(1)}, s32[4]{0:T(128)}, u32[]{:S(2)}) copy-start(s32[4]{0:T(128)} %constant.40.clone) | copy-start | bytes 52
  0.6 16.0 %copy-start.5 = (f32[64,512]{1,0:T(8,128)S(1)}, f32[64,512]{1,0:T(8,128)}, u32[]{:S(2)}) copy-start(f32[64,512]{1,0:T(8,128)} %param.8) | copy-start | bytes 393220
  0.7 18.2 %copy-start.8 = (f32[64,64]{1,0:T(8,128)S(1)}, f32[64,64]{1,0:T(8,128)}, u32[]{:S(2)}) copy-start(f32[64,64]{1,0:T(8,128)} %param.9) | copy-start | bytes 49156
  6.1 14.9 %collective-permute-start = (f32[2,64,512]{2,0,1:T(2,128)S(1)}, f32[2,64,512]{2,0,1:T(2,128)S(1)}, u32[]{:S(2)}, u32[]{:S(2)}) collective-permute-start(f32[2,64,512]{2,0,1:T(2,128)S(1)} %copy.37), channel_id=1, source_target_pairs={{0,4},{4,8},{8,12},{12,16},{16,20},{20,24},{24,28},{1,5},{5,9},{9,... | collective-permute-start | bytes 786440 | tf_op jit(solution)/shard_map/ppermute | solution.py:332
  9.7 11.4 %collective-permute-start.1 = (f32[2,64,512]{2,0,1:T(2,128)S(1)}, f32[2,64,512]{2,0,1:T(2,128)S(1)}, u32[]{:S(2)}, u32[]{:S(2)}) collective-permute-start(f32[2,64,512]{2,0,1:T(2,128)S(1)} %copy.38), channel_id=1, source_target_pairs={{4,0},{8,4},{12,8},{16,12},{20,16},{24,20},{28,24},{5,1},{9,5},{13... | collective-permute-start | bytes 786440 | tf_op jit(solution)/shard_map/ppermute | solution.py:332
  11.0 17.4 %collective-permute-start.2 = (f32[2,4,64,128]{3,2,1,0:T(8,128)}, f32[2,4,64,128]{3,2,1,0:T(8,128)S(1)}, u32[]{:S(2)}, u32[]{:S(2)}) collective-permute-start(f32[2,4,64,128]{3,2,1,0:T(8,128)} %get-tuple-element.20), channel_id=1, source_target_pairs={{0,1},{1,2},{2,3},{4,5},{5,6},{6,7},{8,9},{9,10},{10,11},{12,13},{... | collective-permute-start | bytes 786440 | tf_op jit(solution)/shard_map/ppermute | solution.py:332
  15.3 13.1 %collective-permute-start.3 = (f32[2,4,64,128]{3,2,1,0:T(8,128)}, f32[2,4,64,128]{3,2,1,0:T(8,128)S(1)}, u32[]{:S(2)}, u32[]{:S(2)}) collective-permute-start(f32[2,4,64,128]{3,2,1,0:T(8,128)} %get-tuple-element.21), channel_id=1, source_target_pairs={{1,0},{2,1},{3,2},{5,4},{6,5},{7,6},{9,8},{10,9},{11,10},{13,12},{... | collective-permute-start | bytes 786440 | tf_op jit(solution)/shard_map/ppermute | solution.py:332
  16.6 10.2 %collective-permute-start.6 = (f32[64,512]{1,0:T(8,128)S(1)}, f32[64,512]{1,0:T(8,128)S(1)}, u32[]{:S(2)}, u32[]{:S(2)}) collective-permute-start(f32[64,512]{1,0:T(8,128)S(1)} %copy-done.5), channel_id=1, source_target_pairs={{0,4},{4,0},{8,12},{12,8},{16,20},{20,16},{24,28},{28,24},{1,5},{5... | collective-permute-start | bytes 393224 | tf_op jit(solution)/shard_map/ppermute | solution.py:336
  21.3 7.1 %collective-permute-start.4 = (f32[2,512]{1,0:T(2,128)S(1)}, f32[2,512]{1,0:T(2,128)S(1)}, u32[]{:S(2)}, u32[]{:S(2)}) collective-permute-start(f32[2,512]{1,0:T(2,128)S(1)} %get-tuple-element.43), channel_id=1, source_target_pairs={{0,1},{1,2},{2,3},{4,5},{5,6},{6,7},{8,9},{9,10},{10,11},{12,13},{... | collective-permute-start | bytes 12296 | tf_op jit(solution)/shard_map/ppermute | solution.py:332
  25.5 5.5 %collective-permute-start.5 = (f32[2,512]{1,0:T(2,128)S(1)}, f32[2,512]{1,0:T(2,128)S(1)}, u32[]{:S(2)}, u32[]{:S(2)}) collective-permute-start(f32[2,512]{1,0:T(2,128)S(1)} %get-tuple-element.42), channel_id=1, source_target_pairs={{1,0},{2,1},{3,2},{5,4},{6,5},{7,6},{9,8},{10,9},{11,10},{13,12},{... | collective-permute-start | bytes 12296 | tf_op jit(solution)/shard_map/ppermute | solution.py:332
  40.3 32.8 %collective-permute-start.9 = (f32[16,32,128]{2,1,0:T(8,128)}, f32[16,32,128]{2,1,0:T(8,128)S(1)}, u32[]{:S(2)}, u32[]{:S(2)}) collective-permute-start(f32[16,32,128]{2,1,0:T(8,128)} %get-tuple-element.27), channel_id=1, source_target_pairs={{0,1},{1,0},{2,3},{3,2},{4,5},{5,4},{6,7},{7,6},{8,9},{9,8},{10,11... | collective-permute-start | bytes 786440 | tf_op jit(solution)/shard_map/ppermute | solution.py:336
  41.9 33.9 %collective-permute-start.7 = (f32[128,512]{1,0:T(8,128)S(1)}, f32[128,512]{1,0:T(8,128)S(1)}, u32[]{:S(2)}, u32[]{:S(2)}) collective-permute-start(f32[128,512]{1,0:T(8,128)S(1)} %pad_maximum_fusion.2), channel_id=1, source_target_pairs={{0,8},{4,12},{8,0},{12,4},{16,24},{20,28},{24,16},{28,20},{1,9},{5... | collective-permute-start | bytes 786440 | tf_op jit(solution)/shard_map/ppermute | solution.py:336
  52.9 24.6 %collective-permute-start.11 = (f32[16,32,128]{2,1,0:T(8,128)}, f32[16,32,128]{2,1,0:T(8,128)S(1)}, u32[]{:S(2)}, u32[]{:S(2)}) collective-permute-start(f32[16,32,128]{2,1,0:T(8,128)} %get-tuple-element.29), channel_id=1, source_target_pairs={{0,1},{1,0},{2,3},{3,2},{4,5},{5,4},{6,7},{7,6},{8,9},{9,8},{10,11... | collective-permute-start | bytes 786440 | tf_op jit(solution)/shard_map/ppermute | solution.py:336
  62.2 15.8 %collective-permute-start.13 = (f32[16,32,128]{2,1,0:T(8,128)}, f32[16,32,128]{2,1,0:T(8,128)S(1)}, u32[]{:S(2)}, u32[]{:S(2)}) collective-permute-start(f32[16,32,128]{2,1,0:T(8,128)} %get-tuple-element.31), channel_id=1, source_target_pairs={{0,1},{1,0},{2,3},{3,2},{4,5},{5,4},{6,7},{7,6},{8,9},{9,8},{10,11... | collective-permute-start | bytes 786440 | tf_op jit(solution)/shard_map/ppermute | solution.py:336
  63.8 9.3 %copy-start.4 = (f32[16,32,128]{2,1,0:T(8,128)S(1)}, f32[16,32,128]{2,1,0:T(8,128)}, u32[]{:S(2)}) copy-start(f32[16,32,128]{2,1,0:T(8,128)} %get-tuple-element.26) | copy-start | bytes 786436
  63.8 13.7 %copy-start.3 = (f32[16,32,128]{2,1,0:T(8,128)S(1)}, f32[16,32,128]{2,1,0:T(8,128)}, u32[]{:S(2)}) copy-start(f32[16,32,128]{2,1,0:T(8,128)} %get-tuple-element.28) | copy-start | bytes 786436
  63.8 14.1 %copy-start.2 = (f32[16,32,128]{2,1,0:T(8,128)S(1)}, f32[16,32,128]{2,1,0:T(8,128)}, u32[]{:S(2)}) copy-start(f32[16,32,128]{2,1,0:T(8,128)} %get-tuple-element.30) | copy-start | bytes 786436
  72.6 11.3 %collective-permute-start.15 = (f32[16,32,128]{2,1,0:T(8,128)}, f32[16,32,128]{2,1,0:T(8,128)S(1)}, u32[]{:S(2)}, u32[]{:S(2)}) collective-permute-start(f32[16,32,128]{2,1,0:T(8,128)} %get-tuple-element.33), channel_id=1, source_target_pairs={{0,1},{1,0},{2,3},{3,2},{4,5},{5,4},{6,7},{7,6},{8,9},{9,8},{10,11... | collective-permute-start | bytes 786440 | tf_op jit(solution)/shard_map/ppermute | solution.py:336
  73.1 11.8 %collective-permute-start.10 = (f32[16,16,128]{2,1,0:T(8,128)S(1)}, f32[16,16,128]{2,1,0:T(8,128)S(1)}, u32[]{:S(2)}, u32[]{:S(2)}) collective-permute-start(f32[16,16,128]{2,1,0:T(8,128)S(1)} %slice.53), channel_id=1, source_target_pairs={{0,2},{1,3},{2,0},{3,1},{4,6},{5,7},{6,4},{7,5},{8,10},{9,11},{10,... | collective-permute-start | bytes 393224 | tf_op jit(solution)/shard_map/ppermute | solution.py:336
  75.9 27.6 %collective-permute-start.8 = (f32[256,512]{1,0:T(8,128)S(1)}, f32[256,512]{1,0:T(8,128)S(1)}, u32[]{:S(2)}, u32[]{:S(2)}) collective-permute-start(f32[256,512]{1,0:T(8,128)S(1)} %pad_maximum_fusion), channel_id=1, source_target_pairs={{0,16},{4,20},{8,24},{12,28},{16,0},{20,4},{24,8},{28,12},{1,17},{... | collective-permute-start | bytes 1572872 | tf_op jit(solution)/shard_map/ppermute | solution.py:336
  77.6 17.0 %collective-permute-start.12 = (f32[16,16,128]{2,1,0:T(8,128)S(1)}, f32[16,16,128]{2,1,0:T(8,128)S(1)}, u32[]{:S(2)}, u32[]{:S(2)}) collective-permute-start(f32[16,16,128]{2,1,0:T(8,128)S(1)} %slice.55), channel_id=1, source_target_pairs={{0,2},{1,3},{2,0},{3,1},{4,6},{5,7},{6,4},{7,5},{8,10},{9,11},{10,... | collective-permute-start | bytes 393224 | tf_op jit(solution)/shard_map/ppermute | solution.py:336
  78.0 19.3 %collective-permute-start.14 = (f32[16,16,128]{2,1,0:T(8,128)S(1)}, f32[16,16,128]{2,1,0:T(8,128)S(1)}, u32[]{:S(2)}, u32[]{:S(2)}) collective-permute-start(f32[16,16,128]{2,1,0:T(8,128)S(1)} %slice.57), channel_id=1, source_target_pairs={{0,2},{1,3},{2,0},{3,1},{4,6},{5,7},{6,4},{7,5},{8,10},{9,11},{10,... | collective-permute-start | bytes 393224 | tf_op jit(solution)/shard_map/ppermute | solution.py:336
  84.9 13.9 %collective-permute-start.16 = (f32[16,16,128]{2,1,0:T(8,128)S(1)}, f32[16,16,128]{2,1,0:T(8,128)S(1)}, u32[]{:S(2)}, u32[]{:S(2)}) collective-permute-start(f32[16,16,128]{2,1,0:T(8,128)S(1)} %slice.59), channel_id=1, source_target_pairs={{0,2},{1,3},{2,0},{3,1},{4,6},{5,7},{6,4},{7,5},{8,10},{9,11},{10,... | collective-permute-start | bytes 393224 | tf_op jit(solution)/shard_map/ppermute | solution.py:336
  100.0 13.2 %all-to-all-start = ((f32[8,64,256]{2,1,0:T(8,128)}), f32[8,64,256]{2,1,0:T(8,128)S(1)}, u32[]{:S(2)}, u32[]{:S(2)}) async-start(f32[8,64,256]{2,1,0:T(8,128)} %bitcast.28), calls=%async_computation | async-start | bytes 1048576 | tf_op jit(solution)/shard_map/all_to_all | solution.py:401
  (4 other events, 8.5 us)

commit v2 on v0

v2 whole, which is shorter than its diff:
```python
import functools
import math

import jax
import jax.numpy as jnp
from jax import lax
from jax.experimental import pallas as pl
from jax.experimental.pallas import tpu as pltpu
from jax.sharding import PartitionSpec as P

spread_rate = 0.12
kept_rate = 1.0 - 6.0 * spread_rate
activation = 2.0
exponent = -activation * math.log2(math.e)
lanes = 128
pad = 8
group = 4
f32, bf16 = jnp.float32, jnp.bfloat16
room = pltpu.CompilerParams(vmem_limit_bytes=58 << 20)
in_hbm = pl.BlockSpec(memory_space=pltpu.HBM)
in_vmem = pl.BlockSpec(memory_space=pltpu.VMEM)


def source(field, prefactor):
    return prefactor * jnp.exp2(exponent / (1.0 + field * field))


def along_z(tiles):
    lane = lax.broadcasted_iota(jnp.int32, tiles[0].shape, 1)
    last = len(tiles) - 1
    sums = []
    for k, tile in enumerate(tiles):
        below = tiles[k - 1] if k else 0.0
        above = tiles[k + 1] if k < last else 0.0
        left = pltpu.roll(jnp.where(lane == lanes - 1, below, tile), 1, 1)
        right = pltpu.roll(jnp.where(lane == 0, above, tile), lanes - 1, 1)
        sums.append(left + right)
    return sums


def column(k):
    return slice(k * lanes, (k + 1) * lanes)


def neighbours(buf, slot, count):
    own = [buf[k, slot, pl.ds(pad, count), :] for k in range(buf.shape[0])]
    sums = []
    for k, z_sum in enumerate(along_z(own)):
        beside = buf[k, slot - 1, pl.ds(pad, count), :] + buf[k, slot + 1, pl.ds(pad, count), :]
        beside = beside + (buf[k, slot, pl.ds(pad - 1, count), :] + buf[k, slot, pl.ds(pad + 1, count), :])
        sums.append(beside + z_sum)
    return own, sums


def faces_kernel(peers_y, scalar, prefactor, factor_y, y_lo, y_hi, mix, s_cols, p_cols, line, turned, sems):
    cells_x, cells_y, depth = scalar.shape
    tiles = depth // lanes

    def copies_of(n, source, first_y, buf, side):
        return [
            pltpu.make_async_copy(
                source.at[:, pl.ds(first_y, 8), pl.ds(k * lanes, lanes)],
                buf.at[side, k].reshape(cells_x, 8, lanes),
                sems.at[n, k],
            )
            for k in range(tiles)
        ]

    copies = [
        copies_of(0, scalar, 0, s_cols, 0),
        copies_of(1, prefactor, 0, p_cols, 0),
        copies_of(2, scalar, cells_y - 8, s_cols, 1),
        copies_of(3, prefactor, cells_y - 8, p_cols, 1),
    ]
    for some in copies:
        for one in some:
            one.start()

    ranks = factor_y.shape[1]
    block = ranks // peers_y
    turned[...] = factor_y[...].T
    at_y = lax.axis_index("gy")
    bits = peers_y.bit_length() - 1
    for n in range(peers_y):
        other = int(format(n, f"0{bits}b")[::-1], 2) if bits else 0
        rows = turned[pl.ds(pl.multiple_of((at_y ^ other) * block, block), block), :]
        high = rows.astype(bf16)
        low = (rows - high.astype(f32)).astype(bf16)
        mix[n * block : (n + 1) * block, :] = jnp.concatenate([high, high, low], axis=1)

    for k in range(tiles):
        line[k, 0:pad, :] = jnp.zeros((pad, lanes), f32)
        line[k, pad + cells_x :, :] = jnp.zeros((pad, lanes), f32)
    for side, (out, edge, next_in) in enumerate(((y_lo, 0, 1), (y_hi, 7, 6))):
        for one in copies[2 * side] + copies[2 * side + 1]:
            one.wait()

        def cells(buf, y, k):
            return buf[side, k, pl.ds(y, cells_x, stride=8), :]

        own = [cells(s_cols, edge, k) for k in range(tiles)]
        for k in range(tiles):
            line[k, pad : pad + cells_x, :] = own[k]
        for k, z_sum in enumerate(along_z(own)):
            beside = line[k, pad - 1 : pad - 1 + cells_x, :] + line[k, pad + 1 : pad + 1 + cells_x, :]
            beside = beside + z_sum + cells(s_cols, next_in, k)
            out[0, k] = spread_rate * own[k]
            out[1, k] = spread_rate * beside + (kept_rate * own[k] + source(own[k], cells(p_cols, edge, k)))


def faces(scalar, prefactor, factor_y):
    cells_x, cells_y, depth = scalar.shape
    ranks = factor_y.shape[1]
    face = jax.ShapeDtypeStruct((2, depth // lanes, cells_x, lanes), f32)
    factors = jax.ShapeDtypeStruct((ranks, 3 * cells_y), bf16)
    return pl.pallas_call(
        functools.partial(faces_kernel, lax.axis_size("gy")),
        out_shape=(face, face, factors),
        in_specs=[in_hbm, in_hbm, in_vmem],
        out_specs=[in_vmem] * 3,
        scratch_shapes=[
            pltpu.VMEM((2, depth // lanes, cells_x * 8, lanes), f32),
            pltpu.VMEM((2, depth // lanes, cells_x * 8, lanes), f32),
            pltpu.VMEM((depth // lanes, cells_x + 2 * pad, lanes), f32),
            pltpu.VMEM((ranks, cells_y), f32),
            pltpu.SemaphoreType.DMA((4, depth // lanes)),
        ],
        compiler_params=room,
        name="faces",
    )(scalar, prefactor, factor_y)


def first_kernel(scalar, prefactor, after, middle, s_buf, p_buf, m_buf, s_sem, p_sem, m_sem):
    cells_x, cells_y, depth = scalar.shape
    tiles = depth // lanes
    groups = cells_x // group

    def s_copy(g, k):
        return pltpu.make_async_copy(
            scalar.at[pl.ds(g * group, group), :, pl.ds(k * lanes, lanes)],
            s_buf.at[k, pl.ds(g * group + 1, group), pl.ds(pad, cells_y)],
            s_sem.at[g, k],
        )

    def p_copy(g):
        rows = pl.ds(g * group, group)
        return pltpu.make_async_copy(prefactor.at[rows], p_buf.at[rows], p_sem.at[g])

    def m_copy(g):
        rows = pl.ds(g * group, group)
        return pltpu.make_async_copy(m_buf.at[:, rows], middle.at[:, rows], m_sem.at[g])

    def start(g, carry):
        for k in range(tiles):
            s_copy(g, k).start()
        p_copy(g).start()
        return carry

    lax.fori_loop(0, groups, start, 0)

    for k in range(tiles):
        s_buf[k, 0, pad : pad + cells_y, :] = jnp.zeros((cells_y, lanes), f32)
        s_buf[k, cells_x + 1, pad : pad + cells_y, :] = jnp.zeros((cells_y, lanes), f32)

    def wait_s(g):
        for k in range(tiles):
            s_copy(g, k).wait()

    def row_of(row):
        for k in range(tiles):
            s_buf[k, row + 1, 0:pad, :] = jnp.zeros((pad, lanes), f32)
            s_buf[k, row + 1, pad + cells_y :, :] = jnp.zeros((pad, lanes), f32)
        own, sums = neighbours(s_buf, row + 1, cells_y)
        for k in range(tiles):
            m_buf[k, row] = spread_rate * sums[k] + (kept_rate * own[k] + source(own[k], p_buf[row, :, column(k)]))

    def rows_of(g):
        p_copy(g).wait()

        def one(r, carry):
            row_of(g * group + r)
            return carry

        lax.fori_loop(0, group, one, 0, unroll=True)
        m_copy(g).start()

    wait_s(0)

    def step(g, carry):
        wait_s(g + 1)
        rows_of(g)
        return carry

    lax.fori_loop(0, groups - 1, step, 0)
    rows_of(groups - 1)

    def finish(g, carry):
        m_copy(g).wait()
        return carry

    lax.fori_loop(0, groups, finish, 0)


def first_stage(scalar, prefactor, after):
    cells_x, cells_y, depth = scalar.shape
    tiles, cells = depth // lanes, math.prod(scalar.shape)
    groups = cells_x // group
    return pl.pallas_call(
        first_kernel,
        out_shape=jax.ShapeDtypeStruct((tiles, cells_x, cells_y, lanes), f32),
        in_specs=[in_hbm] * 3,
        out_specs=in_hbm,
        scratch_shapes=[
            pltpu.VMEM((tiles, cells_x + 2, cells_y + 2 * pad, lanes), f32),
            pltpu.VMEM((cells_x, cells_y, depth), f32),
            pltpu.VMEM((tiles, cells_x, cells_y, lanes), f32),
            pltpu.SemaphoreType.DMA((groups, tiles)),
            pltpu.SemaphoreType.DMA((groups,)),
            pltpu.SemaphoreType.DMA((groups,)),
        ],
        cost_estimate=pl.CostEstimate(flops=24 * cells, bytes_accessed=12 * cells, transcendentals=2 * cells),
        compiler_params=room,
        name="first_stage",
    )(scalar, prefactor, after)


def second_kernel(first_row, rows, n_extra, sends, peers, middle, scalar, prefactor, y_lo_in, y_hi_in, factor_z_in, mix_in, *rest):
    (m_buf, s_buf, p_buf, a_buf, low_buf, z_buf, y_lo, y_hi, factor_z, mix, face, m_sem, s_sem, p_sem, a_sem, x_sem, y_sem) = rest[-17:]
    messages = rest[-19:-17] if sends else ()
    (advanced, keep, send) = rest[-22:-19] if sends else rest[-20:-17]
    cells_x, cells_y, depth = scalar.shape
    tiles = depth // lanes
    at_lo, at_hi = first_row == 0, first_row + rows == cells_x
    end = pad + cells_y
    half = keep.shape[1]
    at_x, at_y = lax.axis_index("gx"), lax.axis_index("gy")

    def share(there):
        return jnp.where(there, spread_rate, 0.0).astype(f32)

    y_shares = (share(at_y > 0), share(at_y < peers[1] - 1))

    def m_copy(slot):
        return pltpu.make_async_copy(
            middle.at[:, first_row - 1 + slot], m_buf.at[:, slot, pl.ds(pad, cells_y)], m_sem.at[slot]
        )

    def s_copy(row):
        return pltpu.make_async_copy(scalar.at[first_row + row], s_buf.at[row], s_sem.at[row])

    def p_copy(row):
        return pltpu.make_async_copy(prefactor.at[first_row + row], p_buf.at[row], p_sem.at[row])

    def a_copy(row):
        return pltpu.make_async_copy(a_buf.at[row], advanced.at[first_row + row], a_sem.at[row])

    def start(row, carry):
        m_copy(row + 1).start()
        s_copy(row).start()
        p_copy(row).start()
        return carry

    small = [(y_lo_in, y_lo), (y_hi_in, y_hi), (factor_z_in, factor_z), (mix_in, mix)]
    small += [(rest[0], face)] * n_extra
    small = [pltpu.make_async_copy(a, b, y_sem.at[n]) for n, (a, b) in enumerate(small)]
    if not at_lo:
        m_copy(0).start()
    for row in range(2):
        start(row, 0)
    for copy in small:
        copy.start()
    lax.fori_loop(2, rows, start, 0)
    if not at_hi:
        m_copy(rows + 1).start()

    for copy in small:
        copy.wait()

    x_copies = []
    for n, message in enumerate(messages):
        row = n * (cells_x - 1)
        for k in range(tiles):
            x_copies.append(
                pltpu.make_async_copy(
                    scalar.at[row, :, pl.ds(k * lanes, lanes)], message.at[k, pl.ds(0, cells_y)], x_sem.at[n, k]
                )
            )
            message[k, 2 * cells_y : 2 * cells_y + 1, :] = y_lo[0, k, row : row + 1, :]
            message[k, 2 * cells_y + 1 : 2 * cells_y + 2, :] = y_hi[0, k, row : row + 1, :]
        x_copies.append(
            pltpu.make_async_copy(
                middle.at[:, row], message.at[:, pl.ds(cells_y, cells_y)], x_sem.at[n, tiles]
            )
        )
    for copy in x_copies:
        copy.start()

    def add(k, slot, y, value):
        m_buf[k, slot, pl.ds(y, 1), :] = m_buf[k, slot, pl.ds(y, 1), :] + value

    def settle(slot):
        row = first_row - 1 + slot
        for k in range(tiles):
            add(k, slot, pad, y_lo[0, k, pl.ds(row, 1), :])
            add(k, slot, end - 1, y_hi[0, k, pl.ds(row, 1), :])

    def beside_y(slot):
        row = first_row - 1 + slot
        for k in range(tiles):
            m_buf[k, slot, pad - 1 : pad, :] = (
                y_lo[1, k, pl.ds(row, 1), :] + y_shares[0] * s_buf[slot - 1, 0:1, column(k)]
            )
            m_buf[k, slot, end : end + 1, :] = (
                y_hi[1, k, pl.ds(row, 1), :] + y_shares[1] * s_buf[slot - 1, cells_y - 1 : cells_y, column(k)]
            )

    def edge(there, slot, own_slot):
        part = share(there)
        for k in range(tiles):
            m_buf[k, slot, pad:end, :] = face[k, cells_y : 2 * cells_y, :] + part * s_buf[own_slot - 1, :, column(k)]
            m_buf[k, own_slot, pad:end, :] = m_buf[k, own_slot, pad:end, :] + spread_rate * face[k, :cells_y, :]
            below, above = face[k, 2 * cells_y : 2 * cells_y + 1, :], face[k, 2 * cells_y + 1 : 2 * cells_y + 2, :]
            add(k, slot, pad, below)
            add(k, slot, end - 1, above)
            add(k, own_slot, pad - 1, below)
            add(k, own_slot, end, above)

    def dot_z(row):
        z_buf[row] = jnp.dot(low_buf[row], factor_z[...], preferred_element_type=f32)

    def dot_y(row):
        z = z_buf[row]
        high = z.astype(bf16)
        low = (z - high.astype(f32)).astype(bf16)
        y = jnp.dot(mix[...], jnp.concatenate([high, low, high], axis=0), preferred_element_type=f32)
        keep[row] = y[:half]
        send[row] = y[half:]

    def advance(row):
        slot = row + 1
        own, sums = neighbours(m_buf, slot, cells_y)
        for k in range(tiles):
            value = source(own[k], p_buf[row, :, column(k)]) + s_buf[row, :, column(k)]
            value = 0.5 * (value + (spread_rate * sums[k] + kept_rate * own[k]))
            a_buf[row, :, column(k)] = value
            low_buf[row, :, column(k)] = value.astype(bf16)

    if not at_lo:
        m_copy(0).wait()
        settle(0)
    for row in range(2):
        s_copy(row).wait()
        m_copy(row + 1).wait()
        settle(row + 1)
        beside_y(row + 1)
    if at_lo:
        edge(at_x > 0, 0, 1)

    def step(n, carry):
        t = 2 * n
        for row in (t, t + 1):
            p_copy(row).wait()
            s_copy(row + 2).wait()
            m_copy(row + 3).wait()
        for row in (t, t + 1):
            dot_y(jnp.maximum(row - 4, 0))
        for row in (t, t + 1):
            dot_z(jnp.maximum(row - 2, 0))
        for row in (t, t + 1):
            settle(row + 3)
            beside_y(row + 3)
        for row in (t, t + 1):
            advance(row)
        for row in (t, t + 1):
            a_copy(row).start()
        return carry

    lax.fori_loop(0, rows // 2 - 1, step, 0)
    if at_hi:
        edge(at_x < peers[0] - 1, rows + 1, rows)
    else:
        m_copy(rows + 1).wait()
        settle(rows + 1)
    last = range(rows - 2, rows)
    for row in last:
        p_copy(row).wait()
    for row in last:
        dot_y(row - 4)
    for row in last:
        dot_z(row - 2)
    for row in last:
        advance(row)
    for row in last:
        a_copy(row).start()
    for row in last:
        dot_y(row - 2)
    for row in last:
        dot_z(row)
    for row in last:
        dot_y(row)

    def finish(row, carry):
        a_copy(row).wait()
        return carry

    lax.fori_loop(0, rows, finish, 0)
    for copy in x_copies:
        copy.wait()


def second_stage(first_row, rows, middle, scalar, prefactor, y_lo, y_hi, factor_z, mix, beside, previous, after, sends):
    _, cells_y, depth = scalar.shape
    ranks, z_rank = mix.shape[0], factor_z.shape[1]
    tiles, cells = depth // lanes, rows * cells_y * depth
    part = jax.ShapeDtypeStruct((rows, ranks // 2, z_rank), f32)
    messages = [jax.ShapeDtypeStruct((tiles, 2 * cells_y + pad, lanes), f32)] * (2 * sends)
    operands = [middle, scalar, prefactor, y_lo, y_hi, factor_z, mix, *beside]
    specs = [in_hbm] * (7 + len(beside))
    aliases = {}
    if previous is not None:
        aliases = {len(operands): 0}
        operands.append(previous)
        specs.append(in_hbm)
    operands += after
    specs += [in_hbm] * len(after)
    return pl.pallas_call(
        functools.partial(
            second_kernel, first_row, rows, len(beside), sends, (lax.axis_size("gx"), lax.axis_size("gy"))
        ),
        out_shape=(jax.ShapeDtypeStruct(scalar.shape, f32), part, part, *messages),
        in_specs=specs,
        out_specs=[in_hbm] + [in_vmem] * (2 + len(messages)),
        input_output_aliases=aliases,
        scratch_shapes=[
            pltpu.VMEM((tiles, rows + 2, cells_y + 2 * pad, lanes), f32),
            pltpu.VMEM((rows + 1, cells_y, depth), f32),
            pltpu.VMEM((rows, cells_y, depth), f32),
            pltpu.VMEM((rows, cells_y, depth), f32),
            pltpu.VMEM((rows, cells_y, depth), bf16),
            pltpu.VMEM((rows, cells_y, z_rank), f32),
            pltpu.VMEM(y_lo.shape, f32),
            pltpu.VMEM(y_hi.shape, f32),
            pltpu.VMEM(factor_z.shape, factor_z.dtype),
            pltpu.VMEM(mix.shape, bf16),
            pltpu.VMEM((tiles, 2 * cells_y + pad, lanes), f32),
            pltpu.SemaphoreType.DMA((rows + 2,)),
            pltpu.SemaphoreType.DMA((rows,)),
            pltpu.SemaphoreType.DMA((rows,)),
            pltpu.SemaphoreType.DMA((rows,)),
            pltpu.SemaphoreType.DMA((2, tiles + 1)),
            pltpu.SemaphoreType.DMA((5,)),
        ],
        cost_estimate=pl.CostEstimate(
            flops=30 * cells + 2 * cells * z_rank, bytes_accessed=16 * cells, transcendentals=2 * cells
        ),
        compiler_params=room,
    )(*operands)


def shift(array, axis, step):
    peers = lax.axis_size(axis)
    return lax.ppermute(array, axis, [(i, i + step) for i in range(peers) if 0 <= i + step < peers])


def swap(array, axis, distance):
    return lax.ppermute(array, axis, [(i, i ^ distance) for i in range(lax.axis_size(axis))])


def gathered(array, axis):
    peers = lax.axis_size(axis)
    me, distance, place = lax.axis_index(axis), peers // 2, 0
    while distance:
        other = swap(array, axis, distance)
        upper = (me & distance) != 0
        array = jnp.stack([jnp.where(upper, other, array), jnp.where(upper, array, other)], axis=place)
        distance, place = distance // 2, place + 1
    return array.reshape((-1,) + array.shape[-1:])


def runs_of(cells_x):
    eighth = cells_x // 8
    return [(eighth, 4 * eighth), (5 * eighth, 3 * eighth), (0, eighth)]


def on_device(scalar, prefactor, factor_x, factor_y, factor_z):
    cells_x, _, _ = scalar.shape
    peers_x, peers_y = lax.axis_size("gx"), lax.axis_size("gy")
    y_rank, z_rank = factor_y.shape[1], factor_z.shape[1]
    block = y_rank // peers_y

    to_y_lo, to_y_hi, mix = faces(scalar, prefactor, factor_y)
    y_lo, y_hi = shift(to_y_hi, "gy", 1), shift(to_y_lo, "gy", -1)
    middle = first_stage(scalar, prefactor, to_y_lo)

    def halved(run):
        number, held, coming, distance = run
        held = held + coming
        if 2 * distance == peers_y:
            owned[number] = held
            return []
        half = held.shape[1] // 2
        coming = swap(held[:, half:], "gy", 2 * distance)
        return [(number, held[:, :half], coming, 2 * distance)]

    all_x = gathered(factor_x, "gx")
    runs = runs_of(cells_x)
    advanced, owned, in_flight = None, {}, []
    for number, (first_row, rows) in enumerate(runs):
        beside = [x_lo] * (first_row == 0) + [x_hi] * (first_row + rows == cells_x) if number else []
        advanced, keep, send, *messages = second_stage(
            first_row, rows, middle, scalar, prefactor, y_lo, y_hi, factor_z, mix, beside, advanced, [], not number
        )
        in_flight = sum((halved(run) for run in in_flight), [])
        in_flight.append((number, keep, swap(send, "gy", 1), 1))
        if messages:
            x_lo = shift(messages[1], "gx", 1)
            x_hi = shift(messages[0], "gx", -1)
    while in_flight:
        in_flight = sum((halved(run) for run in in_flight), [])
    owned = jnp.concatenate([owned[number] for number in sorted(owned, key=lambda n: runs[n][0])], axis=0)

    columns = block * z_rank // peers_x
    parts = owned.reshape(cells_x, peers_x, columns).transpose(1, 0, 2)
    parts = lax.all_to_all(parts, "gx", 0, 0, tiled=True).reshape(peers_x * cells_x, columns)
    core = jnp.einsum("xa,xn->an", all_x, parts, precision=lax.Precision.HIGHEST)
    core = core.reshape(peers_x, -1, columns)
    core = lax.all_to_all(core, "gx", 0, 0, tiled=True)
    core = core.transpose(1, 0, 2).reshape(-1, block, z_rank)
    return (advanced, core)


def solution(mesh):
    return jax.shard_map(
        on_device,
        mesh=mesh,
        in_specs=(P("gx", "gy", None), P("gx", "gy", None), P("gx", None), P("gy", None), P()),
        out_specs=(P("gx", "gy", None), P("gx", "gy", None)),
        check_vma=False,
    )
```

time: 267 us -> 119 us (0.45)
  other arithmetic: 87.3 us -> 1.51 us
  waiting for transfers between devices: 96.5 us -> 36.3 us
  Pallas kernels: 0 us -> 36.4 us
  local copies, waits for them, and re-layouts: 32.1 us -> 4.85 us
  between operations: 14.2 us -> 0.94 us
  matrix products: 14.1 us -> 0.98 us
  blocking collectives: 0 us -> 12.1 us
  starting transfers between devices: 21.9 us -> 25.2 us
    reduce_scatter x2 -> x0, waiting for transfers between devices: 90.8 us -> none  [the longest x1 52.1 us: on_device(): y_owned = lax.psum_scatter(y_reduced, 'gy', scatter_dimension=1, tiled=True)]
    convert_element_type x1 -> x0, other arithmetic: 44.1 us -> none  [on_device(): lowered = advanced.astype(jnp.bfloat16)]
    add x1 -> x6, other arithmetic: 42.2 us -> 1.14 us  [halved(): held = held + coming]
    pallas_call x0 -> x5, Pallas kernels: none -> 36.4 us  [the longest x3 22 us: second_stage(): pl.pallas_call(functools.partial(second_kernel, first_row, rows, len(besi...]
    ppermute x8 -> x13, waiting for transfers between devices: 5.71 us -> 27.2 us  [the longest x9 27.2 us: swap(): lax.ppermute(array, axis, [(i, i ^ distance) for i in range(lax.axis_size...]
    unnamed x10 -> x16, local copies, waits for them, and re-layouts: 23.2 us -> 2.24 us
    dot_general x3 -> x1, matrix products: 14.1 us -> 0.98 us  [on_device(): jnp.einsum('xa,xn->an', all_x, parts, precision=lax.Precision.HIGHEST)]
    all_to_all x0 -> x1, blocking collectives: none -> 12.1 us  [on_device(): core = lax.all_to_all(core, 'gx', 0, 0, tiled=True)]
  transfers between devices with their start and end apart: 10 -> 14, of which waited for: 7 -> 6; matrix products, arithmetic and copies ran while one was open for 8% -> 3% of each run, Pallas kernels for 0% -> 23%
where the time goes in v2:
time: 119 us; the launch traced here: 118 us
  Pallas kernels  36.4 us (31%)
  waiting for transfers between devices  36.3 us (31%)
  starting transfers between devices  25.2 us (21%)
  blocking collectives  12.1 us (10%)
  local copies, waits for them, and re-layouts  4.85 us (4%)
  other arithmetic  1.51 us (1%)
    ppermute x9, waiting for transfers between devices, swap(): lax.ppermute(array, axis, [(i, i ^ distance) for i in range(lax.axis_size...  27.2 us
    pallas_call x3, Pallas kernels, second_stage(): pl.pallas_call(functools.partial(second_kernel, first_row, rows, len(besi...  22 us
    all_to_all x1, blocking collectives, on_device(): core = lax.all_to_all(core, 'gx', 0, 0, tiled=True)  12.1 us
    ppermute x9, starting transfers between devices, swap(): lax.ppermute(array, axis, [(i, i ^ distance) for i in range(lax.axis_size...  11.5 us
    pallas_call x1, Pallas kernels, first_stage(): pl.pallas_call(first_kernel, out_shape=jax.ShapeDtypeStruct((tiles, cells...  10.5 us
    ppermute x4, starting transfers between devices, shift(): lax.ppermute(array, axis, [(i, i + step) for i in range(peers) if 0 <= i...  10.2 us
    all_to_all x1, waiting for transfers between devices, on_device(): lax.all_to_all(parts, 'gx', 0, 0, tiled=True)  9.06 us
    pallas_call x1, Pallas kernels, faces(): pl.pallas_call(functools.partial(faces_kernel, lax.axis_size('gy')), out_...  3.97 us
  transfers between devices with their start and end apart: 14, of which 6 were waited for; matrix products, arithmetic and copies ran while one was open for 3% of the time, Pallas kernels for 23%

profile of v2, /device:TPU:0, one launch (start us, length us, event | category | flops | bytes accessed | tf_op | source)
XLA Modules:
  0.0 118.3 jit_solution(7568748091827262995)
XLA Ops:
  0.6 3.1 %collective-permute-start.4 = (f32[64,512]{1,0:T(8,128)}, f32[64,512]{1,0:T(8,128)S(1)}, u32[]{:S(2)}, u32[]{:S(2)}) collective-permute-start(f32[64,512]{1,0:T(8,128)} %param.7), channel_id=1, source_target_pairs={{0,16},{4,20},{8,24},{12,28},{16,0},{20,4},{24,8},{28,12},{1,17},{... | collective-permute-start | bytes 393224 | tf_op jit(solution)/shard_map/ppermute | solution.py:466
  3.7 4.0 %faces.1 = (f32[2,4,64,128]{3,2,1,0:T(8,128)}, f32[2,4,64,128]{3,2,1,0:T(8,128)}, bf16[64,192]{1,0:T(8,128)(2,1)}) custom-call(f32[64,64,512]{2,1,0:T(8,128)} %scalar.9, f32[64,64,512]{2,1,0:T(8,128)} %prefactor.9, f32[64,64]{1,0:T(8,128)} %factor_y.1), custom_call_target="tpu_custom_call" | custom-call | tf_op jit(solution)/shard_map/faces/pallas_call | solution.py:116
  7.7 1.3 %collective-permute-start.1 = (f32[2,4,64,128]{3,2,1,0:T(8,128)}, f32[2,4,64,128]{3,2,1,0:T(8,128)S(1)}, u32[]{:S(2)}, u32[]{:S(2)}) collective-permute-start(f32[2,4,64,128]{3,2,1,0:T(8,128)} %get-tuple-element.16.after), channel_id=1, source_target_pairs={{1,0},{2,1},{3,2},{5,4},{6,5},{7,6},{9,8},{10,9},{11,10},{13,12},{... | collective-permute-start | bytes 786440 | tf_op jit(solution)/shard_map/ppermute | solution.py:462
  9.0 4.6 %collective-permute-start = (f32[2,4,64,128]{3,2,1,0:T(8,128)}, f32[2,4,64,128]{3,2,1,0:T(8,128)S(1)}, u32[]{:S(2)}, u32[]{:S(2)}) collective-permute-start(f32[2,4,64,128]{3,2,1,0:T(8,128)} %get-tuple-element.17), channel_id=1, source_target_pairs={{0,1},{1,2},{2,3},{4,5},{5,6},{6,7},{8,9},{9,10},{10,11},{12,13},{... | collective-permute-start | bytes 786440 | tf_op jit(solution)/shard_map/ppermute | solution.py:462
  13.6 10.5 %first_stage.1.middle = f32[4,64,64,128]{3,2,1,0:T(8,128)} custom-call(f32[64,64,512]{2,1,0:T(8,128)} %scalar.9, f32[64,64,512]{2,1,0:T(8,128)} %prefactor.9, f32[2,4,64,128]{3,2,1,0:T(8,128)} %get-tuple-element.16.after), custom_call_target="tpu_custom_call" | custom-call | flops 50331648 | bytes 25165824 | tf_op jit(solution)/shard_map/first_stage/pallas_call | solution.py:208
  24.9 9.6 %shard_map.68 = (f32[64,64,512]{2,1,0:T(8,128)}, f32[32,32,128]{2,1,0:T(8,128)}, f32[32,32,128]{2,1,0:T(8,128)}, f32[4,136,128]{2,1,0:T(8,128)}, f32[4,136,128]{2,1,0:T(8,128)}) custom-call(f32[4,64,64,128]{3,2,1,0:T(8,128)} %first_stage.1.middle, f32[64,64,512]{2,1,0:T(8,128)} %scalar.9, f32[64,64,512]{2,1,0:T(8,128)} %prefactor.9, ...), custom_call_target="tpu_custom_call" | custom-call | flops 299892736 | bytes 16777216 | tf_op jit(solution)/shard_map/pallas_call | solution.py:426
  34.5 1.3 %collective-permute-start.3 = (f32[4,136,128]{2,1,0:T(8,128)}, f32[4,136,128]{2,1,0:T(8,128)S(1)}, u32[]{:S(2)}, u32[]{:S(2)}) collective-permute-start(f32[4,136,128]{2,1,0:T(8,128)} %get-tuple-element.20), channel_id=1, source_target_pairs={{4,0},{8,4},{12,8},{16,12},{20,16},{24,20},{28,24},{5,1},{9,5},{13... | collective-permute-start | bytes 835592 | tf_op jit(solution)/shard_map/ppermute | solution.py:462
  35.8 3.0 %collective-permute-start.2 = (f32[4,136,128]{2,1,0:T(8,128)}, f32[4,136,128]{2,1,0:T(8,128)S(1)}, u32[]{:S(2)}, u32[]{:S(2)}) collective-permute-start(f32[4,136,128]{2,1,0:T(8,128)} %get-tuple-element.19), channel_id=1, source_target_pairs={{0,4},{4,8},{8,12},{12,16},{16,20},{20,24},{24,28},{1,5},{5,9},{9,... | collective-permute-start | bytes 835592 | tf_op jit(solution)/shard_map/ppermute | solution.py:462
  38.9 1.6 %collective-permute-start.9 = (f32[32,32,128]{2,1,0:T(8,128)}, f32[32,32,128]{2,1,0:T(8,128)S(1)}, u32[]{:S(2)}, u32[]{:S(2)}) collective-permute-start(f32[32,32,128]{2,1,0:T(8,128)} %get-tuple-element.27), channel_id=1, source_target_pairs={{0,1},{1,0},{2,3},{3,2},{4,5},{5,4},{6,7},{7,6},{8,9},{9,8},{10,11... | collective-permute-start | bytes 1572872 | tf_op jit(solution)/shard_map/ppermute | solution.py:466
  40.5 1.5 %collective-permute-start.5 = (f32[2,64,512]{2,1,0:T(8,128)S(1)}, f32[2,64,512]{2,1,0:T(8,128)S(1)}, u32[]{:S(2)}, u32[]{:S(2)}) collective-permute-start(f32[2,64,512]{2,1,0:T(8,128)S(1)} %pad_maximum_fusion.3), channel_id=1, source_target_pairs={{0,8},{4,12},{8,0},{12,4},{16,24},{20,28},{24,16},{28,20},{1,9},{5... | collective-permute-start | bytes 786440 | tf_op jit(solution)/shard_map/ppermute | solution.py:466
  42.7 7.7 %shard_map.69 = (f32[64,64,512]{2,1,0:T(8,128)}, f32[24,32,128]{2,1,0:T(8,128)}, f32[24,32,128]{2,1,0:T(8,128)}) custom-call(f32[4,64,64,128]{3,2,1,0:T(8,128)} %first_stage.1.middle, f32[64,64,512]{2,1,0:T(8,128)} %scalar.9, f32[64,64,512]{2,1,0:T(8,128)} %prefactor.9, f32[2,4,64,128]{3,2,1,0:T(8,128)} %copy-done.1, ...), custom_call_target="tpu_custom_call", output_to_operand_aliasing={{0}: (8, {})} | custom-call | flops 224919552 | bytes 12582912 | tf_op jit(solution)/shard_map/pallas_call | solution.py:426
  51.2 4.7 %shard_map.70 = (f32[64,64,512]{2,1,0:T(8,128)}, f32[8,32,128]{2,1,0:T(8,128)}, f32[8,32,128]{2,1,0:T(8,128)}) custom-call(f32[4,64,64,128]{3,2,1,0:T(8,128)} %first_stage.1.middle, f32[64,64,512]{2,1,0:T(8,128)} %scalar.9, f32[64,64,512]{2,1,0:T(8,128)} %prefactor.9, f32[2,4,64,128]{3,2,1,0:T(8,128)} %copy-done.1, ...), custom_call_target="tpu_custom_call", output_to_operand_aliasing={{0}: (8, {})} | custom-call | flops 74973184 | bytes 4194304 | tf_op jit(solution)/shard_map/pallas_call | solution.py:426
  56.5 1.5 %collective-permute-start.11 = (f32[24,32,128]{2,1,0:T(8,128)S(1)}, f32[24,32,128]{2,1,0:T(8,128)S(1)}, u32[]{:S(2)}, u32[]{:S(2)}) collective-permute-start(f32[24,32,128]{2,1,0:T(8,128)S(1)} %copy-done.7), channel_id=1, source_target_pairs={{0,1},{1,0},{2,3},{3,2},{4,5},{5,4},{6,7},{7,6},{8,9},{9,8},{10,11... | collective-permute-start | bytes 1179656 | tf_op jit(solution)/shard_map/ppermute | solution.py:466
  58.0 4.5 %collective-permute-done.7 = f32[8,32,128]{2,1,0:T(8,128)S(1)} collective-permute-done((f32[8,32,128]{2,1,0:T(8,128)}, f32[8,32,128]{2,1,0:T(8,128)S(1)}, u32[]{:S(2)}, u32[]{:S(2)}) %collective-permute-start.7) | collective-permute-done | bytes 131104 | tf_op jit(solution)/shard_map/ppermute | solution.py:466
  64.3 2.3 %collective-permute-start.10 = (f32[32,16,128]{2,1,0:T(8,128)S(1)}, f32[32,16,128]{2,1,0:T(8,128)S(1)}, u32[]{:S(2)}, u32[]{:S(2)}) collective-permute-start(f32[32,16,128]{2,1,0:T(8,128)S(1)} %slice.27), channel_id=1, source_target_pairs={{0,2},{1,3},{2,0},{3,1},{4,6},{5,7},{6,4},{7,5},{8,10},{9,11},{10,... | collective-permute-start | bytes 786440 | tf_op jit(solution)/shard_map/ppermute | solution.py:466
  66.8 2.7 %collective-permute-done.8 = f32[8,16,128]{2,1,0:T(8,128)S(1)} collective-permute-done((f32[8,16,128]{2,1,0:T(8,128)S(1)}, f32[8,16,128]{2,1,0:T(8,128)S(1)}, u32[]{:S(2)}, u32[]{:S(2)}) %collective-permute-start.8) | collective-permute-done | bytes 65568 | tf_op jit(solution)/shard_map/ppermute | solution.py:466
  69.5 5.5 %collective-permute-done.11 = f32[24,32,128]{2,1,0:T(8,128)S(1)} collective-permute-done((f32[24,32,128]{2,1,0:T(8,128)S(1)}, f32[24,32,128]{2,1,0:T(8,128)S(1)}, u32[]{:S(2)}, u32[]{:S(2)}) %collective-permute-start.11) | collective-permute-done | bytes 393248 | tf_op jit(solution)/shard_map/ppermute | solution.py:466
  75.1 10.4 %collective-permute-done.10 = f32[32,16,128]{2,1,0:T(8,128)S(1)} collective-permute-done((f32[32,16,128]{2,1,0:T(8,128)S(1)}, f32[32,16,128]{2,1,0:T(8,128)S(1)}, u32[]{:S(2)}, u32[]{:S(2)}) %collective-permute-start.10) | collective-permute-done | bytes 262176 | tf_op jit(solution)/shard_map/ppermute | solution.py:466
  85.5 4.2 %collective-permute-done.12 = f32[24,16,128]{2,1,0:T(8,128)S(1)} collective-permute-done((f32[24,16,128]{2,1,0:T(8,128)S(1)}, f32[24,16,128]{2,1,0:T(8,128)S(1)}, u32[]{:S(2)}, u32[]{:S(2)}) %collective-permute-start.12) | collective-permute-done | bytes 196640 | tf_op jit(solution)/shard_map/ppermute | solution.py:466
  89.9 1.0 copy.21
  90.9 3.5 %all-to-all-start = ((f32[8,64,256]{2,1,0:T(8,128)}), f32[8,64,256]{2,1,0:T(8,128)S(1)}, u32[]{:S(2)}, u32[]{:S(2)}) async-start(f32[8,64,256]{2,1,0:T(8,128)} %bitcast.28), calls=%async_computation | async-start | bytes 1048576 | tf_op jit(solution)/shard_map/all_to_all | solution.py:524
  95.0 9.1 %all-to-all-done = f32[8,64,256]{2,1,0:T(8,128)S(1)} async-done(((f32[8,64,256]{2,1,0:T(8,128)}), f32[8,64,256]{2,1,0:T(8,128)S(1)}, u32[]{:S(2)}, u32[]{:S(2)}) %all-to-all-start) | async-done | bytes 524320 | tf_op jit(solution)/shard_map/all_to_all | solution.py:524
  104.0 1.0 fusion
  105.0 12.1 %all_to_all.10 = f32[8,64,256]{2,1,0:T(8,128)S(1)} all-to-all(f32[8,64,256]{2,1,0:T(8,128)S(1)} %fusion), channel_id=1, replica_groups=mesh['gx'=8,'gy'=4] {'gx'}, dimensions={0} | all-to-all | bytes 1048576 | tf_op jit(solution)/shard_map/all_to_all | solution.py:527
  (48 shorter events, 6.9 us)
Async XLA Ops:
  0.6 23.4 %collective-permute-start.4 = (f32[64,512]{1,0:T(8,128)}, f32[64,512]{1,0:T(8,128)S(1)}, u32[]{:S(2)}, u32[]{:S(2)}) collective-permute-start(f32[64,512]{1,0:T(8,128)} %param.7), channel_id=1, source_target_pairs={{0,16},{4,20},{8,24},{12,28},{16,0},{20,4},{24,8},{28,12},{1,17},{... | collective-permute-start | bytes 393224 | tf_op jit(solution)/shard_map/ppermute | solution.py:466
  7.7 16.4 %collective-permute-start.1 = (f32[2,4,64,128]{3,2,1,0:T(8,128)}, f32[2,4,64,128]{3,2,1,0:T(8,128)S(1)}, u32[]{:S(2)}, u32[]{:S(2)}) collective-permute-start(f32[2,4,64,128]{3,2,1,0:T(8,128)} %get-tuple-element.16.after), channel_id=1, source_target_pairs={{1,0},{2,1},{3,2},{5,4},{6,5},{7,6},{9,8},{10,9},{11,10},{13,12},{... | collective-permute-start | bytes 786440 | tf_op jit(solution)/shard_map/ppermute | solution.py:462
  9.0 15.1 %collective-permute-start = (f32[2,4,64,128]{3,2,1,0:T(8,128)}, f32[2,4,64,128]{3,2,1,0:T(8,128)S(1)}, u32[]{:S(2)}, u32[]{:S(2)}) collective-permute-start(f32[2,4,64,128]{3,2,1,0:T(8,128)} %get-tuple-element.17), channel_id=1, source_target_pairs={{0,1},{1,2},{2,3},{4,5},{5,6},{6,7},{8,9},{9,10},{10,11},{12,13},{... | collective-permute-start | bytes 786440 | tf_op jit(solution)/shard_map/ppermute | solution.py:462
  13.5 10.5 %copy-start.6 = (f32[64,512]{1,0:T(8,128)S(1)}, f32[64,512]{1,0:T(8,128)}, u32[]{:S(2)}) copy-start(f32[64,512]{1,0:T(8,128)} %param.7) | copy-start | bytes 393220
  24.1 0.7 copy-start
  24.1 0.8 copy-start.1
  34.5 7.5 %collective-permute-start.3 = (f32[4,136,128]{2,1,0:T(8,128)}, f32[4,136,128]{2,1,0:T(8,128)S(1)}, u32[]{:S(2)}, u32[]{:S(2)}) collective-permute-start(f32[4,136,128]{2,1,0:T(8,128)} %get-tuple-element.20), channel_id=1, source_target_pairs={{4,0},{8,4},{12,8},{16,12},{20,16},{24,20},{28,24},{5,1},{9,5},{13... | collective-permute-start | bytes 835592 | tf_op jit(solution)/shard_map/ppermute | solution.py:462
  35.8 14.7 %collective-permute-start.2 = (f32[4,136,128]{2,1,0:T(8,128)}, f32[4,136,128]{2,1,0:T(8,128)S(1)}, u32[]{:S(2)}, u32[]{:S(2)}) collective-permute-start(f32[4,136,128]{2,1,0:T(8,128)} %get-tuple-element.19), channel_id=1, source_target_pairs={{0,4},{4,8},{8,12},{12,16},{16,20},{20,24},{24,28},{1,5},{5,9},{9,... | collective-permute-start | bytes 835592 | tf_op jit(solution)/shard_map/ppermute | solution.py:462
  38.9 25.4 %collective-permute-start.9 = (f32[32,32,128]{2,1,0:T(8,128)}, f32[32,32,128]{2,1,0:T(8,128)S(1)}, u32[]{:S(2)}, u32[]{:S(2)}) collective-permute-start(f32[32,32,128]{2,1,0:T(8,128)} %get-tuple-element.27), channel_id=1, source_target_pairs={{0,1},{1,0},{2,3},{3,2},{4,5},{5,4},{6,7},{7,6},{8,9},{9,8},{10,11... | collective-permute-start | bytes 1572872 | tf_op jit(solution)/shard_map/ppermute | solution.py:466
  40.5 17.5 %collective-permute-start.5 = (f32[2,64,512]{2,1,0:T(8,128)S(1)}, f32[2,64,512]{2,1,0:T(8,128)S(1)}, u32[]{:S(2)}, u32[]{:S(2)}) collective-permute-start(f32[2,64,512]{2,1,0:T(8,128)S(1)} %pad_maximum_fusion.3), channel_id=1, source_target_pairs={{0,8},{4,12},{8,0},{12,4},{16,24},{20,28},{24,16},{28,20},{1,9},{5... | collective-permute-start | bytes 786440 | tf_op jit(solution)/shard_map/ppermute | solution.py:466
  42.0 0.7 copy-start.5
  50.5 0.7 copy-start.4
  51.2 5.2 %copy-start.7 = (f32[24,32,128]{2,1,0:T(8,128)S(1)}, f32[24,32,128]{2,1,0:T(8,128)}, u32[]{:S(2)}) copy-start(f32[24,32,128]{2,1,0:T(8,128)} %get-tuple-element.29) | copy-start | bytes 1179652
  51.2 13.0 %copy-start.2 = (f32[32,32,128]{2,1,0:T(8,128)S(1)}, f32[32,32,128]{2,1,0:T(8,128)}, u32[]{:S(2)}) copy-start(f32[32,32,128]{2,1,0:T(8,128)} %get-tuple-element.26) | copy-start | bytes 1572868
  51.2 23.7 %copy-start.3 = (f32[24,32,128]{2,1,0:T(8,128)S(1)}, f32[24,32,128]{2,1,0:T(8,128)}, u32[]{:S(2)}) copy-start(f32[24,32,128]{2,1,0:T(8,128)} %get-tuple-element.28) | copy-start | bytes 1179652
  55.9 6.6 %collective-permute-start.7 = (f32[8,32,128]{2,1,0:T(8,128)}, f32[8,32,128]{2,1,0:T(8,128)S(1)}, u32[]{:S(2)}, u32[]{:S(2)}) collective-permute-start(f32[8,32,128]{2,1,0:T(8,128)} %get-tuple-element.25), channel_id=1, source_target_pairs={{0,1},{1,0},{2,3},{3,2},{4,5},{5,4},{6,7},{7,6},{8,9},{9,8},{10,11... | collective-permute-start | bytes 393224 | tf_op jit(solution)/shard_map/ppermute | solution.py:466
  56.5 18.5 %collective-permute-start.11 = (f32[24,32,128]{2,1,0:T(8,128)S(1)}, f32[24,32,128]{2,1,0:T(8,128)S(1)}, u32[]{:S(2)}, u32[]{:S(2)}) collective-permute-start(f32[24,32,128]{2,1,0:T(8,128)S(1)} %copy-done.7), channel_id=1, source_target_pairs={{0,1},{1,0},{2,3},{3,2},{4,5},{5,4},{6,7},{7,6},{8,9},{9,8},{10,11... | collective-permute-start | bytes 1179656 | tf_op jit(solution)/shard_map/ppermute | solution.py:466
  63.5 6.0 %collective-permute-start.8 = (f32[8,16,128]{2,1,0:T(8,128)S(1)}, f32[8,16,128]{2,1,0:T(8,128)S(1)}, u32[]{:S(2)}, u32[]{:S(2)}) collective-permute-start(f32[8,16,128]{2,1,0:T(8,128)S(1)} %slice.25), channel_id=1, source_target_pairs={{0,2},{1,3},{2,0},{3,1},{4,6},{5,7},{6,4},{7,5},{8,10},{9,11},{10,... | collective-permute-start | bytes 196616 | tf_op jit(solution)/shard_map/ppermute | solution.py:466
  64.3 21.1 %collective-permute-start.10 = (f32[32,16,128]{2,1,0:T(8,128)S(1)}, f32[32,16,128]{2,1,0:T(8,128)S(1)}, u32[]{:S(2)}, u32[]{:S(2)}) collective-permute-start(f32[32,16,128]{2,1,0:T(8,128)S(1)} %slice.27), channel_id=1, source_target_pairs={{0,2},{1,3},{2,0},{3,1},{4,6},{5,7},{6,4},{7,5},{8,10},{9,11},{10,... | collective-permute-start | bytes 786440 | tf_op jit(solution)/shard_map/ppermute | solution.py:466
  66.7 27.7 %collective-permute-start.6 = (f32[2,2,64,512]{3,2,1,0:T(8,128)S(1)}, f32[2,2,64,512]{3,2,1,0:T(8,128)S(1)}, u32[]{:S(2)}, u32[]{:S(2)}) collective-permute-start(f32[2,2,64,512]{3,2,1,0:T(8,128)S(1)} %pad_maximum_fusion.1), channel_id=1, source_target_pairs={{0,4},{4,0},{8,12},{12,8},{16,20},{20,16},{24,28},{28,24},{1,5},{5... | collective-permute-start | bytes 1572872 | tf_op jit(solution)/shard_map/ppermute | solution.py:466
  75.0 14.6 %collective-permute-start.12 = (f32[24,16,128]{2,1,0:T(8,128)S(1)}, f32[24,16,128]{2,1,0:T(8,128)S(1)}, u32[]{:S(2)}, u32[]{:S(2)}) collective-permute-start(f32[24,16,128]{2,1,0:T(8,128)S(1)} %slice.29), channel_id=1, source_target_pairs={{0,2},{1,3},{2,0},{3,1},{4,6},{5,7},{6,4},{7,5},{8,10},{9,11},{10,... | collective-permute-start | bytes 589832 | tf_op jit(solution)/shard_map/ppermute | solution.py:466
  90.9 13.2 %all-to-all-start = ((f32[8,64,256]{2,1,0:T(8,128)}), f32[8,64,256]{2,1,0:T(8,128)S(1)}, u32[]{:S(2)}, u32[]{:S(2)}) async-start(f32[8,64,256]{2,1,0:T(8,128)} %bitcast.28), calls=%async_computation | async-start | bytes 1048576 | tf_op jit(solution)/shard_map/all_to_all | solution.py:524

commit v3 on v2

--- a/solution.py
+++ b/solution.py
@@ -13,6 +13,7 @@
 activation = 2.0
 exponent = -activation * math.log2(math.e)
 lanes = 128
+piece = 32
 pad = 8
 group = 4
 f32, bf16 = jnp.float32, jnp.bfloat16
@@ -42,14 +43,24 @@
     return slice(k * lanes, (k + 1) * lanes)
 
 
-def neighbours(buf, slot, count):
-    own = [buf[k, slot, pl.ds(pad, count), :] for k in range(buf.shape[0])]
-    sums = []
-    for k, z_sum in enumerate(along_z(own)):
-        beside = buf[k, slot - 1, pl.ds(pad, count), :] + buf[k, slot + 1, pl.ds(pad, count), :]
-        beside = beside + (buf[k, slot, pl.ds(pad - 1, count), :] + buf[k, slot, pl.ds(pad + 1, count), :])
-        sums.append(beside + z_sum)
-    return own, sums
+def beside_z(tile, below, above):
+    lane = lax.broadcasted_iota(jnp.int32, tile.shape, 1)
+    left = pltpu.roll(jnp.where(lane == lanes - 1, below, tile), 1, 1)
+    right = pltpu.roll(jnp.where(lane == 0, above, tile), lanes - 1, 1)
+    return left + right
+
+
+def neighbours(buf, slot, k, first, count):
+    def cells(k, slot, y):
+        return buf[k, slot, pl.ds(pad + y, count), :]
+
+    own = cells(k, slot, first)
+    below = cells(k - 1, slot, first) if k else 0.0
+    above = cells(k + 1, slot, first) if k < buf.shape[0] - 1 else 0.0
+    beside = (cells(k, slot - 1, first) + cells(k, slot + 1, first)) + (
+        cells(k, slot, first - 1) + cells(k, slot, first + 1)
+    )
+    return own, beside + beside_z(own, below, above)
 
 
 def faces_kernel(peers_y, scalar, prefactor, factor_y, y_lo, y_hi, mix, s_cols, p_cols, line, turned, sems):
@@ -162,17 +173,26 @@
         s_buf[k, 0, pad : pad + cells_y, :] = jnp.zeros((cells_y, lanes), f32)
         s_buf[k, cells_x + 1, pad : pad + cells_y, :] = jnp.zeros((cells_y, lanes), f32)
 
-    def wait_s(g):
-        for k in range(tiles):
-            s_copy(g, k).wait()
-
-    def row_of(row):
+    def clear(row, carry):
         for k in range(tiles):
             s_buf[k, row + 1, 0:pad, :] = jnp.zeros((pad, lanes), f32)
             s_buf[k, row + 1, pad + cells_y :, :] = jnp.zeros((pad, lanes), f32)
-        own, sums = neighbours(s_buf, row + 1, cells_y)
-        for k in range(tiles):
-            m_buf[k, row] = spread_rate * sums[k] + (kept_rate * own[k] + source(own[k], p_buf[row, :, column(k)]))
+        return carry
+
+    lax.fori_loop(0, cells_x, clear, 0)
+
+    def wait_s(g):
+        for k in range(tiles):
+            s_copy(g, k).wait()
+
+    pieces = [(k, y) for k in range(tiles) for y in range(0, cells_y, piece)]
+
+    def row_of(row):
+        for k, y in pieces:
+            own, beside = neighbours(s_buf, row + 1, k, y, piece)
+            m_buf[k, row, pl.ds(y, piece), :] = spread_rate * beside + (
+                kept_rate * own + source(own, p_buf[row, pl.ds(y, piece), column(k)])
+            )
 
     def rows_of(g):
         p_copy(g).wait()
@@ -265,11 +285,11 @@
     small = [pltpu.make_async_copy(a, b, y_sem.at[n]) for n, (a, b) in enumerate(small)]
     if not at_lo:
         m_copy(0).start()
-    for row in range(2):
+    for row in range(3):
         start(row, 0)
     for copy in small:
         copy.start()
-    lax.fori_loop(2, rows, start, 0)
+    lax.fori_loop(3, rows, start, 0)
     if not at_hi:
         m_copy(rows + 1).start()
 
@@ -336,60 +356,69 @@
         keep[row] = y[:half]
         send[row] = y[half:]
 
+    pieces = [(k, y) for k in range(tiles) for y in range(0, cells_y, piece)]
+
     def advance(row):
         slot = row + 1
-        own, sums = neighbours(m_buf, slot, cells_y)
-        for k in range(tiles):
-            value = source(own[k], p_buf[row, :, column(k)]) + s_buf[row, :, column(k)]
-            value = 0.5 * (value + (spread_rate * sums[k] + kept_rate * own[k]))
-            a_buf[row, :, column(k)] = value
-            low_buf[row, :, column(k)] = value.astype(bf16)
-
-    if not at_lo:
-        m_copy(0).wait()
-        settle(0)
-    for row in range(2):
+        for k, y in pieces:
+            own, beside = neighbours(m_buf, slot, k, y, piece)
+            value = source(own, p_buf[row, pl.ds(y, piece), column(k)]) + s_buf[row, pl.ds(y, piece), column(k)]
+            value = 0.5 * (value + (spread_rate * beside + kept_rate * own))
+            a_buf[row, pl.ds(y, piece), column(k)] = value
+            low_buf[row, pl.ds(y, piece), column(k)] = value.astype(bf16)
+
+    for slot in range(4):
+        if slot or not at_lo:
+            m_copy(slot).wait()
+    for row in range(3):
         s_copy(row).wait()
-        m_copy(row + 1).wait()
-        settle(row + 1)
-        beside_y(row + 1)
+    for slot in range(4):
+        if slot or not at_lo:
+            settle(slot)
+        if slot:
+            beside_y(slot)
     if at_lo:
         edge(at_x > 0, 0, 1)
 
-    def step(n, carry):
-        t = 2 * n
+    def forward(t):
         for row in (t, t + 1):
             p_copy(row).wait()
-            s_copy(row + 2).wait()
-            m_copy(row + 3).wait()
         for row in (t, t + 1):
             dot_y(jnp.maximum(row - 4, 0))
         for row in (t, t + 1):
             dot_z(jnp.maximum(row - 2, 0))
         for row in (t, t + 1):
-            settle(row + 3)
-            beside_y(row + 3)
-        for row in (t, t + 1):
             advance(row)
+
+    def step(n, carry):
+        t = 2 * n
+        for slot in (t + 4, t + 5):
+            s_copy(slot - 1).wait()
+            m_copy(slot).wait()
+        forward(t)
+        for slot in (t + 4, t + 5):
+            settle(slot)
+            beside_y(slot)
         for row in (t, t + 1):
             a_copy(row).start()
         return carry
 
-    lax.fori_loop(0, rows // 2 - 1, step, 0)
+    lax.fori_loop(0, rows // 2 - 2, step, 0)
+    s_copy(rows - 1).wait()
+    m_copy(rows).wait()
+    if not at_hi:
+        m_copy(rows + 1).wait()
+    forward(rows - 4)
+    settle(rows)
+    beside_y(rows)
     if at_hi:
         edge(at_x < peers[0] - 1, rows + 1, rows)
     else:
-        m_copy(rows + 1).wait()
         settle(rows + 1)
-    last = range(rows - 2, rows)
-    for row in last:
-        p_copy(row).wait()
-    for row in last:
-        dot_y(row - 4)
-    for row in last:
-        dot_z(row - 2)
-    for row in last:
-        advance(row)
+    for row in (rows - 4, rows - 3):
+        a_copy(row).start()
+    last = (rows - 2, rows - 1)
+    forward(rows - 2)
     for row in last:
         a_copy(row).start()
     for row in last:
@@ -478,8 +507,8 @@
 
 
 def runs_of(cells_x):
-    eighth = cells_x // 8
-    return [(eighth, 4 * eighth), (5 * eighth, 3 * eighth), (0, eighth)]
+    part = cells_x // 16
+    return [(2 * part, 9 * part), (11 * part, 5 * part), (0, 2 * part)]
 
 
 def on_device(scalar, prefactor, factor_x, factor_y, factor_z):

time: 119 us -> 119 us (level)
  transfers between devices with their start and end apart: 14 -> 14, of which waited for: 6 -> 4; matrix products, arithmetic and copies ran while one was open for 3% -> 3% of each run, Pallas kernels for 23% -> 22%
where the time goes in v3:
time: 119 us
  Pallas kernels  36.5 us (31%)
  waiting for transfers between devices  36.5 us (31%)
  starting transfers between devices  25.4 us (21%)
  blocking collectives  12.1 us (10%)
  local copies, waits for them, and re-layouts  4.84 us (4%)
  other arithmetic  1.52 us (1%)
    ppermute x9, waiting for transfers between devices, swap(): lax.ppermute(array, axis, [(i, i ^ distance) for i in range(lax.axis_size...  27.5 us
    pallas_call x3, Pallas kernels, second_stage(): pl.pallas_call(functools.partial(second_kernel, first_row, rows, len(besi...  22 us
    all_to_all x1, blocking collectives, on_device(): core = lax.all_to_all(core, 'gx', 0, 0, tiled=True)  12.1 us
    ppermute x9, starting transfers between devices, swap(): lax.ppermute(array, axis, [(i, i ^ distance) for i in range(lax.axis_size...  11.8 us
    pallas_call x1, Pallas kernels, first_stage(): pl.pallas_call(first_kernel, out_shape=jax.ShapeDtypeStruct((tiles, cells...  10.5 us
    ppermute x4, starting transfers between devices, shift(): lax.ppermute(array, axis, [(i, i + step) for i in range(peers) if 0 <= i...  10.2 us
    all_to_all x1, waiting for transfers between devices, on_device(): lax.all_to_all(parts, 'gx', 0, 0, tiled=True)  9.06 us
    pallas_call x1, Pallas kernels, faces(): pl.pallas_call(functools.partial(faces_kernel, lax.axis_size('gy')), out_...  3.97 us
  transfers between devices with their start and end apart: 14, of which 4 were waited for; matrix products, arithmetic and copies ran while one was open for 3% of the time, Pallas kernels for 22%

profile of v3, /device:TPU:0, one launch (start us, length us, event | category | flops | bytes accessed | tf_op | source)
XLA Modules:
  0.0 118.9 jit_solution(13874155295303481293)
XLA Ops:
  0.6 3.1 %collective-permute-start.4 = (f32[64,512]{1,0:T(8,128)}, f32[64,512]{1,0:T(8,128)S(1)}, u32[]{:S(2)}, u32[]{:S(2)}) collective-permute-start(f32[64,512]{1,0:T(8,128)} %param.7), channel_id=1, source_target_pairs={{0,16},{4,20},{8,24},{12,28},{16,0},{20,4},{24,8},{28,12},{1,17},{... | collective-permute-start | bytes 393224 | tf_op jit(solution)/shard_map/ppermute | solution.py:495
  3.7 4.0 %faces.1 = (f32[2,4,64,128]{3,2,1,0:T(8,128)}, f32[2,4,64,128]{3,2,1,0:T(8,128)}, bf16[64,192]{1,0:T(8,128)(2,1)}) custom-call(f32[64,64,512]{2,1,0:T(8,128)} %scalar.9, f32[64,64,512]{2,1,0:T(8,128)} %prefactor.9, f32[64,64]{1,0:T(8,128)} %factor_y.1), custom_call_target="tpu_custom_call" | custom-call | tf_op jit(solution)/shard_map/faces/pallas_call | solution.py:127
  7.7 1.3 %collective-permute-start.1 = (f32[2,4,64,128]{3,2,1,0:T(8,128)}, f32[2,4,64,128]{3,2,1,0:T(8,128)S(1)}, u32[]{:S(2)}, u32[]{:S(2)}) collective-permute-start(f32[2,4,64,128]{3,2,1,0:T(8,128)} %get-tuple-element.16.after), channel_id=1, source_target_pairs={{1,0},{2,1},{3,2},{5,4},{6,5},{7,6},{9,8},{10,9},{11,10},{13,12},{... | collective-permute-start | bytes 786440 | tf_op jit(solution)/shard_map/ppermute | solution.py:491
  9.0 4.6 %collective-permute-start = (f32[2,4,64,128]{3,2,1,0:T(8,128)}, f32[2,4,64,128]{3,2,1,0:T(8,128)S(1)}, u32[]{:S(2)}, u32[]{:S(2)}) collective-permute-start(f32[2,4,64,128]{3,2,1,0:T(8,128)} %get-tuple-element.17), channel_id=1, source_target_pairs={{0,1},{1,2},{2,3},{4,5},{5,6},{6,7},{8,9},{9,10},{10,11},{12,13},{... | collective-permute-start | bytes 786440 | tf_op jit(solution)/shard_map/ppermute | solution.py:491
  13.6 10.5 %first_stage.1.middle = f32[4,64,64,128]{3,2,1,0:T(8,128)} custom-call(f32[64,64,512]{2,1,0:T(8,128)} %scalar.9, f32[64,64,512]{2,1,0:T(8,128)} %prefactor.9, f32[2,4,64,128]{3,2,1,0:T(8,128)} %get-tuple-element.16.after), custom_call_target="tpu_custom_call" | custom-call | flops 50331648 | bytes 25165824 | tf_op jit(solution)/shard_map/first_stage/pallas_call | solution.py:228
  24.9 10.4 %shard_map.68 = (f32[64,64,512]{2,1,0:T(8,128)}, f32[36,32,128]{2,1,0:T(8,128)}, f32[36,32,128]{2,1,0:T(8,128)}, f32[4,136,128]{2,1,0:T(8,128)}, f32[4,136,128]{2,1,0:T(8,128)}) custom-call(f32[4,64,64,128]{3,2,1,0:T(8,128)} %first_stage.1.middle, f32[64,64,512]{2,1,0:T(8,128)} %scalar.9, f32[64,64,512]{2,1,0:T(8,128)} %prefactor.9, ...), custom_call_target="tpu_custom_call" | custom-call | flops 337379328 | bytes 18874368 | tf_op jit(solution)/shard_map/pallas_call | solution.py:455
  35.3 1.3 %collective-permute-start.3 = (f32[4,136,128]{2,1,0:T(8,128)}, f32[4,136,128]{2,1,0:T(8,128)S(1)}, u32[]{:S(2)}, u32[]{:S(2)}) collective-permute-start(f32[4,136,128]{2,1,0:T(8,128)} %get-tuple-element.20), channel_id=1, source_target_pairs={{4,0},{8,4},{12,8},{16,12},{20,16},{24,20},{28,24},{5,1},{9,5},{13... | collective-permute-start | bytes 835592 | tf_op jit(solution)/shard_map/ppermute | solution.py:491
  36.6 3.0 %collective-permute-start.2 = (f32[4,136,128]{2,1,0:T(8,128)}, f32[4,136,128]{2,1,0:T(8,128)S(1)}, u32[]{:S(2)}, u32[]{:S(2)}) collective-permute-start(f32[4,136,128]{2,1,0:T(8,128)} %get-tuple-element.19), channel_id=1, source_target_pairs={{0,4},{4,8},{8,12},{12,16},{16,20},{20,24},{24,28},{1,5},{5,9},{9,... | collective-permute-start | bytes 835592 | tf_op jit(solution)/shard_map/ppermute | solution.py:491
  39.7 1.5 %collective-permute-start.5 = (f32[2,64,512]{2,1,0:T(8,128)S(1)}, f32[2,64,512]{2,1,0:T(8,128)S(1)}, u32[]{:S(2)}, u32[]{:S(2)}) collective-permute-start(f32[2,64,512]{2,1,0:T(8,128)S(1)} %pad_maximum_fusion.3), channel_id=1, source_target_pairs={{0,8},{4,12},{8,0},{12,4},{16,24},{20,28},{24,16},{28,20},{1,9},{5... | collective-permute-start | bytes 786440 | tf_op jit(solution)/shard_map/ppermute | solution.py:495
  41.2 1.6 %collective-permute-start.9 = (f32[36,32,128]{2,1,0:T(8,128)}, f32[36,32,128]{2,1,0:T(8,128)S(1)}, u32[]{:S(2)}, u32[]{:S(2)}) collective-permute-start(f32[36,32,128]{2,1,0:T(8,128)} %get-tuple-element.27), channel_id=1, source_target_pairs={{0,1},{1,0},{2,3},{3,2},{4,5},{5,4},{6,7},{7,6},{8,9},{9,8},{10,11... | collective-permute-start | bytes 1769480 | tf_op jit(solution)/shard_map/ppermute | solution.py:495
  43.5 6.9 %shard_map.69 = (f32[64,64,512]{2,1,0:T(8,128)}, f32[20,32,128]{2,1,0:T(8,128)}, f32[20,32,128]{2,1,0:T(8,128)}) custom-call(f32[4,64,64,128]{3,2,1,0:T(8,128)} %first_stage.1.middle, f32[64,64,512]{2,1,0:T(8,128)} %scalar.9, f32[64,64,512]{2,1,0:T(8,128)} %prefactor.9, f32[2,4,64,128]{3,2,1,0:T(8,128)} %copy-done.1, ...), custom_call_target="tpu_custom_call", output_to_operand_aliasing={{0}: (8, {})} | custom-call | flops 187432960 | bytes 10485760 | tf_op jit(solution)/shard_map/pallas_call | solution.py:455
  51.2 4.7 %shard_map.70 = (f32[64,64,512]{2,1,0:T(8,128)}, f32[8,32,128]{2,1,0:T(8,128)}, f32[8,32,128]{2,1,0:T(8,128)}) custom-call(f32[4,64,64,128]{3,2,1,0:T(8,128)} %first_stage.1.middle, f32[64,64,512]{2,1,0:T(8,128)} %scalar.9, f32[64,64,512]{2,1,0:T(8,128)} %prefactor.9, f32[2,4,64,128]{3,2,1,0:T(8,128)} %copy-done.1, ...), custom_call_target="tpu_custom_call", output_to_operand_aliasing={{0}: (8, {})} | custom-call | flops 74973184 | bytes 4194304 | tf_op jit(solution)/shard_map/pallas_call | solution.py:455
  56.4 1.6 %collective-permute-start.11 = (f32[20,32,128]{2,1,0:T(8,128)S(1)}, f32[20,32,128]{2,1,0:T(8,128)S(1)}, u32[]{:S(2)}, u32[]{:S(2)}) collective-permute-start(f32[20,32,128]{2,1,0:T(8,128)S(1)} %copy-done.7), channel_id=1, source_target_pairs={{0,1},{1,0},{2,3},{3,2},{4,5},{5,4},{6,7},{7,6},{8,9},{9,8},{10,11... | collective-permute-start | bytes 983048 | tf_op jit(solution)/shard_map/ppermute | solution.py:495
  58.1 4.5 %collective-permute-done.7 = f32[8,32,128]{2,1,0:T(8,128)S(1)} collective-permute-done((f32[8,32,128]{2,1,0:T(8,128)}, f32[8,32,128]{2,1,0:T(8,128)S(1)}, u32[]{:S(2)}, u32[]{:S(2)}) %collective-permute-start.7) | collective-permute-done | bytes 131104 | tf_op jit(solution)/shard_map/ppermute | solution.py:495
  62.6 0.9 add.18
  64.3 1.2 %collective-permute-start.6 = (f32[2,2,64,512]{3,2,1,0:T(8,128)S(1)}, f32[2,2,64,512]{3,2,1,0:T(8,128)S(1)}, u32[]{:S(2)}, u32[]{:S(2)}) collective-permute-start(f32[2,2,64,512]{3,2,1,0:T(8,128)S(1)} %pad_maximum_fusion.1), channel_id=1, source_target_pairs={{0,4},{4,0},{8,12},{12,8},{16,20},{20,16},{24,28},{28,24},{1,5},{5... | collective-permute-start | bytes 1572872 | tf_op jit(solution)/shard_map/ppermute | solution.py:495
  65.7 1.2 collective-permute-start.10
  66.8 4.8 %collective-permute-done.11 = f32[20,32,128]{2,1,0:T(8,128)S(1)} collective-permute-done((f32[20,32,128]{2,1,0:T(8,128)S(1)}, f32[20,32,128]{2,1,0:T(8,128)S(1)}, u32[]{:S(2)}, u32[]{:S(2)}) %collective-permute-start.11) | collective-permute-done | bytes 327712 | tf_op jit(solution)/shard_map/ppermute | solution.py:495
  72.0 18.2 %collective-permute-done.12 = f32[20,16,128]{2,1,0:T(8,128)S(1)} collective-permute-done((f32[20,16,128]{2,1,0:T(8,128)S(1)}, f32[20,16,128]{2,1,0:T(8,128)S(1)}, u32[]{:S(2)}, u32[]{:S(2)}) %collective-permute-start.12) | collective-permute-done | bytes 163872 | tf_op jit(solution)/shard_map/ppermute | solution.py:495
  90.5 1.0 copy.21
  91.5 3.5 %all-to-all-start = ((f32[8,64,256]{2,1,0:T(8,128)}), f32[8,64,256]{2,1,0:T(8,128)S(1)}, u32[]{:S(2)}, u32[]{:S(2)}) async-start(f32[8,64,256]{2,1,0:T(8,128)} %bitcast.28), calls=%async_computation | async-start | bytes 1048576 | tf_op jit(solution)/shard_map/all_to_all | solution.py:553
  95.6 9.1 %all-to-all-done = f32[8,64,256]{2,1,0:T(8,128)S(1)} async-done(((f32[8,64,256]{2,1,0:T(8,128)}), f32[8,64,256]{2,1,0:T(8,128)S(1)}, u32[]{:S(2)}, u32[]{:S(2)}) %all-to-all-start) | async-done | bytes 524320 | tf_op jit(solution)/shard_map/all_to_all | solution.py:553
  104.6 1.0 fusion
  105.6 12.1 %all_to_all.10 = f32[8,64,256]{2,1,0:T(8,128)S(1)} all-to-all(f32[8,64,256]{2,1,0:T(8,128)S(1)} %fusion), channel_id=1, replica_groups=mesh['gx'=8,'gy'=4] {'gx'}, dimensions={0} | all-to-all | bytes 1048576 | tf_op jit(solution)/shard_map/all_to_all | solution.py:556
  (48 shorter events, 6.1 us)
Async XLA Ops:
  0.6 23.4 %collective-permute-start.4 = (f32[64,512]{1,0:T(8,128)}, f32[64,512]{1,0:T(8,128)S(1)}, u32[]{:S(2)}, u32[]{:S(2)}) collective-permute-start(f32[64,512]{1,0:T(8,128)} %param.7), channel_id=1, source_target_pairs={{0,16},{4,20},{8,24},{12,28},{16,0},{20,4},{24,8},{28,12},{1,17},{... | collective-permute-start | bytes 393224 | tf_op jit(solution)/shard_map/ppermute | solution.py:495
  7.7 16.4 %collective-permute-start.1 = (f32[2,4,64,128]{3,2,1,0:T(8,128)}, f32[2,4,64,128]{3,2,1,0:T(8,128)S(1)}, u32[]{:S(2)}, u32[]{:S(2)}) collective-permute-start(f32[2,4,64,128]{3,2,1,0:T(8,128)} %get-tuple-element.16.after), channel_id=1, source_target_pairs={{1,0},{2,1},{3,2},{5,4},{6,5},{7,6},{9,8},{10,9},{11,10},{13,12},{... | collective-permute-start | bytes 786440 | tf_op jit(solution)/shard_map/ppermute | solution.py:491
  9.0 15.1 %collective-permute-start = (f32[2,4,64,128]{3,2,1,0:T(8,128)}, f32[2,4,64,128]{3,2,1,0:T(8,128)S(1)}, u32[]{:S(2)}, u32[]{:S(2)}) collective-permute-start(f32[2,4,64,128]{3,2,1,0:T(8,128)} %get-tuple-element.17), channel_id=1, source_target_pairs={{0,1},{1,2},{2,3},{4,5},{5,6},{6,7},{8,9},{9,10},{10,11},{12,13},{... | collective-permute-start | bytes 786440 | tf_op jit(solution)/shard_map/ppermute | solution.py:491
  13.5 10.5 %copy-start.6 = (f32[64,512]{1,0:T(8,128)S(1)}, f32[64,512]{1,0:T(8,128)}, u32[]{:S(2)}) copy-start(f32[64,512]{1,0:T(8,128)} %param.7) | copy-start | bytes 393220
  24.1 0.7 copy-start
  24.1 0.8 copy-start.1
  35.3 7.5 %collective-permute-start.3 = (f32[4,136,128]{2,1,0:T(8,128)}, f32[4,136,128]{2,1,0:T(8,128)S(1)}, u32[]{:S(2)}, u32[]{:S(2)}) collective-permute-start(f32[4,136,128]{2,1,0:T(8,128)} %get-tuple-element.20), channel_id=1, source_target_pairs={{4,0},{8,4},{12,8},{16,12},{20,16},{24,20},{28,24},{5,1},{9,5},{13... | collective-permute-start | bytes 835592 | tf_op jit(solution)/shard_map/ppermute | solution.py:491
  36.6 13.8 %collective-permute-start.2 = (f32[4,136,128]{2,1,0:T(8,128)}, f32[4,136,128]{2,1,0:T(8,128)S(1)}, u32[]{:S(2)}, u32[]{:S(2)}) collective-permute-start(f32[4,136,128]{2,1,0:T(8,128)} %get-tuple-element.19), channel_id=1, source_target_pairs={{0,4},{4,8},{8,12},{12,16},{16,20},{20,24},{24,28},{1,5},{5,9},{9,... | collective-permute-start | bytes 835592 | tf_op jit(solution)/shard_map/ppermute | solution.py:491
  39.7 18.3 %collective-permute-start.5 = (f32[2,64,512]{2,1,0:T(8,128)S(1)}, f32[2,64,512]{2,1,0:T(8,128)S(1)}, u32[]{:S(2)}, u32[]{:S(2)}) collective-permute-start(f32[2,64,512]{2,1,0:T(8,128)S(1)} %pad_maximum_fusion.3), channel_id=1, source_target_pairs={{0,8},{4,12},{8,0},{12,4},{16,24},{20,28},{24,16},{28,20},{1,9},{5... | collective-permute-start | bytes 786440 | tf_op jit(solution)/shard_map/ppermute | solution.py:495
  41.2 24.3 %collective-permute-start.9 = (f32[36,32,128]{2,1,0:T(8,128)}, f32[36,32,128]{2,1,0:T(8,128)S(1)}, u32[]{:S(2)}, u32[]{:S(2)}) collective-permute-start(f32[36,32,128]{2,1,0:T(8,128)} %get-tuple-element.27), channel_id=1, source_target_pairs={{0,1},{1,0},{2,3},{3,2},{4,5},{5,4},{6,7},{7,6},{8,9},{9,8},{10,11... | collective-permute-start | bytes 1769480 | tf_op jit(solution)/shard_map/ppermute | solution.py:495
  42.8 0.7 copy-start.5
  50.5 0.7 copy-start.4
  51.2 5.2 %copy-start.7 = (f32[20,32,128]{2,1,0:T(8,128)S(1)}, f32[20,32,128]{2,1,0:T(8,128)}, u32[]{:S(2)}) copy-start(f32[20,32,128]{2,1,0:T(8,128)} %get-tuple-element.29) | copy-start | bytes 983044
  51.2 14.3 %copy-start.2 = (f32[36,32,128]{2,1,0:T(8,128)S(1)}, f32[36,32,128]{2,1,0:T(8,128)}, u32[]{:S(2)}) copy-start(f32[36,32,128]{2,1,0:T(8,128)} %get-tuple-element.26) | copy-start | bytes 1769476
  51.2 20.4 %copy-start.3 = (f32[20,32,128]{2,1,0:T(8,128)S(1)}, f32[20,32,128]{2,1,0:T(8,128)}, u32[]{:S(2)}) copy-start(f32[20,32,128]{2,1,0:T(8,128)} %get-tuple-element.28) | copy-start | bytes 983044
  55.9 6.6 %collective-permute-start.7 = (f32[8,32,128]{2,1,0:T(8,128)}, f32[8,32,128]{2,1,0:T(8,128)S(1)}, u32[]{:S(2)}, u32[]{:S(2)}) collective-permute-start(f32[8,32,128]{2,1,0:T(8,128)} %get-tuple-element.25), channel_id=1, source_target_pairs={{0,1},{1,0},{2,3},{3,2},{4,5},{5,4},{6,7},{7,6},{8,9},{9,8},{10,11... | collective-permute-start | bytes 393224 | tf_op jit(solution)/shard_map/ppermute | solution.py:495
  56.4 15.2 %collective-permute-start.11 = (f32[20,32,128]{2,1,0:T(8,128)S(1)}, f32[20,32,128]{2,1,0:T(8,128)S(1)}, u32[]{:S(2)}, u32[]{:S(2)}) collective-permute-start(f32[20,32,128]{2,1,0:T(8,128)S(1)} %copy-done.7), channel_id=1, source_target_pairs={{0,1},{1,0},{2,3},{3,2},{4,5},{5,4},{6,7},{7,6},{8,9},{9,8},{10,11... | collective-permute-start | bytes 983048 | tf_op jit(solution)/shard_map/ppermute | solution.py:495
  63.5 8.5 %collective-permute-start.8 = (f32[8,16,128]{2,1,0:T(8,128)S(1)}, f32[8,16,128]{2,1,0:T(8,128)S(1)}, u32[]{:S(2)}, u32[]{:S(2)}) collective-permute-start(f32[8,16,128]{2,1,0:T(8,128)S(1)} %slice.25), channel_id=1, source_target_pairs={{0,2},{1,3},{2,0},{3,1},{4,6},{5,7},{6,4},{7,5},{8,10},{9,11},{10,... | collective-permute-start | bytes 196616 | tf_op jit(solution)/shard_map/ppermute | solution.py:495
  64.3 30.7 %collective-permute-start.6 = (f32[2,2,64,512]{3,2,1,0:T(8,128)S(1)}, f32[2,2,64,512]{3,2,1,0:T(8,128)S(1)}, u32[]{:S(2)}, u32[]{:S(2)}) collective-permute-start(f32[2,2,64,512]{3,2,1,0:T(8,128)S(1)} %pad_maximum_fusion.1), channel_id=1, source_target_pairs={{0,4},{4,0},{8,12},{12,8},{16,20},{20,16},{24,28},{28,24},{1,5},{5... | collective-permute-start | bytes 1572872 | tf_op jit(solution)/shard_map/ppermute | solution.py:495
  65.7 24.6 %collective-permute-start.10 = (f32[36,16,128]{2,1,0:T(8,128)S(1)}, f32[36,16,128]{2,1,0:T(8,128)S(1)}, u32[]{:S(2)}, u32[]{:S(2)}) collective-permute-start(f32[36,16,128]{2,1,0:T(8,128)S(1)} %slice.27), channel_id=1, source_target_pairs={{0,2},{1,3},{2,0},{3,1},{4,6},{5,7},{6,4},{7,5},{8,10},{9,11},{10,... | collective-permute-start | bytes 884744 | tf_op jit(solution)/shard_map/ppermute | solution.py:495
  71.7 18.5 %collective-permute-start.12 = (f32[20,16,128]{2,1,0:T(8,128)S(1)}, f32[20,16,128]{2,1,0:T(8,128)S(1)}, u32[]{:S(2)}, u32[]{:S(2)}) collective-permute-start(f32[20,16,128]{2,1,0:T(8,128)S(1)} %slice.29), channel_id=1, source_target_pairs={{0,2},{1,3},{2,0},{3,1},{4,6},{5,7},{6,4},{7,5},{8,10},{9,11},{10,... | collective-permute-start | bytes 491528 | tf_op jit(solution)/shard_map/ppermute | solution.py:495
  91.5 13.2 %all-to-all-start = ((f32[8,64,256]{2,1,0:T(8,128)}), f32[8,64,256]{2,1,0:T(8,128)S(1)}, u32[]{:S(2)}, u32[]{:S(2)}) async-start(f32[8,64,256]{2,1,0:T(8,128)} %bitcast.28), calls=%async_computation | async-start | bytes 1048576 | tf_op jit(solution)/shard_map/all_to_all | solution.py:553

commit v4 on v3

--- a/solution.py
+++ b/solution.py
@@ -15,7 +15,7 @@
 lanes = 128
 piece = 32
 pad = 8
-group = 4
+group = 8
 f32, bf16 = jnp.float32, jnp.bfloat16
 room = pltpu.CompilerParams(vmem_limit_bytes=58 << 20)
 in_hbm = pl.BlockSpec(memory_space=pltpu.HBM)
@@ -546,12 +546,11 @@
             x_hi = shift(messages[0], "gx", -1)
     while in_flight:
         in_flight = sum((halved(run) for run in in_flight), [])
-    owned = jnp.concatenate([owned[number] for number in sorted(owned, key=lambda n: runs[n][0])], axis=0)
-
     columns = block * z_rank // peers_x
-    parts = owned.reshape(cells_x, peers_x, columns).transpose(1, 0, 2)
+    parts = [owned[n].reshape(-1, peers_x, columns).transpose(1, 0, 2) for n in sorted(owned, key=lambda n: runs[n][0])]
+    parts = jnp.concatenate(parts, axis=1)
     parts = lax.all_to_all(parts, "gx", 0, 0, tiled=True).reshape(peers_x * cells_x, columns)
-    core = jnp.einsum("xa,xn->an", all_x, parts, precision=lax.Precision.HIGHEST)
+    core = jnp.einsum("xa,xn->an", all_x, parts, precision=lax.Precision.HIGH)
     core = core.reshape(peers_x, -1, columns)
     core = lax.all_to_all(core, "gx", 0, 0, tiled=True)
     core = core.transpose(1, 0, 2).reshape(-1, block, z_rank)

time: 119 us -> 119 us (level)
  other arithmetic: 1.52 us -> 3.14 us
where the time goes in v4:
time: 119 us
  Pallas kernels  36 us (30%)
  waiting for transfers between devices  35.9 us (30%)
  starting transfers between devices  25.9 us (22%)
  blocking collectives  12.1 us (10%)
  local copies, waits for them, and re-layouts  4.07 us (3%)
  other arithmetic  3.14 us (3%)
    ppermute x9, waiting for transfers between devices, swap(): lax.ppermute(array, axis, [(i, i ^ distance) for i in range(lax.axis_size...  26.8 us
    pallas_call x3, Pallas kernels, second_stage(): pl.pallas_call(functools.partial(second_kernel, first_row, rows, len(besi...  22 us
    all_to_all x1, blocking collectives, on_device(): core = lax.all_to_all(core, 'gx', 0, 0, tiled=True)  12.1 us
    ppermute x9, starting transfers between devices, swap(): lax.ppermute(array, axis, [(i, i ^ distance) for i in range(lax.axis_size...  11.9 us
    ppermute x4, starting transfers between devices, shift(): lax.ppermute(array, axis, [(i, i + step) for i in range(peers) if 0 <= i...  10.2 us
    pallas_call x1, Pallas kernels, first_stage(): pl.pallas_call(first_kernel, out_shape=jax.ShapeDtypeStruct((tiles, cells...  10 us
    all_to_all x1, waiting for transfers between devices, on_device(): lax.all_to_all(parts, 'gx', 0, 0, tiled=True)  9.12 us
    pallas_call x1, Pallas kernels, faces(): pl.pallas_call(functools.partial(faces_kernel, lax.axis_size('gy')), out_...  3.97 us
  transfers between devices with their start and end apart: 14, of which 4 were waited for; matrix products, arithmetic and copies ran while one was open for 3% of the time, Pallas kernels for 22%

profile of v4, /device:TPU:0, one launch (start us, length us, event | category | flops | bytes accessed | tf_op | source)
XLA Modules:
  0.0 118.7 jit_solution(3168152892323127844)
XLA Ops:
  0.6 3.1 %collective-permute-start.4 = (f32[64,512]{1,0:T(8,128)}, f32[64,512]{1,0:T(8,128)S(1)}, u32[]{:S(2)}, u32[]{:S(2)}) collective-permute-start(f32[64,512]{1,0:T(8,128)} %param.7), channel_id=1, source_target_pairs={{0,16},{4,20},{8,24},{12,28},{16,0},{20,4},{24,8},{28,12},{1,17},{... | collective-permute-start | bytes 393224 | tf_op jit(solution)/shard_map/ppermute | solution.py:495
  3.7 4.0 %faces.1 = (f32[2,4,64,128]{3,2,1,0:T(8,128)}, f32[2,4,64,128]{3,2,1,0:T(8,128)}, bf16[64,192]{1,0:T(8,128)(2,1)}) custom-call(f32[64,64,512]{2,1,0:T(8,128)} %scalar.9, f32[64,64,512]{2,1,0:T(8,128)} %prefactor.9, f32[64,64]{1,0:T(8,128)} %factor_y.1), custom_call_target="tpu_custom_call" | custom-call | tf_op jit(solution)/shard_map/faces/pallas_call | solution.py:127
  7.7 1.3 %collective-permute-start.1 = (f32[2,4,64,128]{3,2,1,0:T(8,128)}, f32[2,4,64,128]{3,2,1,0:T(8,128)S(1)}, u32[]{:S(2)}, u32[]{:S(2)}) collective-permute-start(f32[2,4,64,128]{3,2,1,0:T(8,128)} %get-tuple-element.16.after), channel_id=1, source_target_pairs={{1,0},{2,1},{3,2},{5,4},{6,5},{7,6},{9,8},{10,9},{11,10},{13,12},{... | collective-permute-start | bytes 786440 | tf_op jit(solution)/shard_map/ppermute | solution.py:491
  9.0 4.6 %collective-permute-start = (f32[2,4,64,128]{3,2,1,0:T(8,128)}, f32[2,4,64,128]{3,2,1,0:T(8,128)S(1)}, u32[]{:S(2)}, u32[]{:S(2)}) collective-permute-start(f32[2,4,64,128]{3,2,1,0:T(8,128)} %get-tuple-element.17), channel_id=1, source_target_pairs={{0,1},{1,2},{2,3},{4,5},{5,6},{6,7},{8,9},{9,10},{10,11},{12,13},{... | collective-permute-start | bytes 786440 | tf_op jit(solution)/shard_map/ppermute | solution.py:491
  13.6 10.0 %first_stage.1.middle = f32[4,64,64,128]{3,2,1,0:T(8,128)} custom-call(f32[64,64,512]{2,1,0:T(8,128)} %scalar.9, f32[64,64,512]{2,1,0:T(8,128)} %prefactor.9, f32[2,4,64,128]{3,2,1,0:T(8,128)} %get-tuple-element.16.after), custom_call_target="tpu_custom_call" | custom-call | flops 50331648 | bytes 25165824 | tf_op jit(solution)/shard_map/first_stage/pallas_call | solution.py:228
  24.4 10.4 %shard_map.68 = (f32[64,64,512]{2,1,0:T(8,128)}, f32[36,32,128]{2,1,0:T(8,128)}, f32[36,32,128]{2,1,0:T(8,128)}, f32[4,136,128]{2,1,0:T(8,128)}, f32[4,136,128]{2,1,0:T(8,128)}) custom-call(f32[4,64,64,128]{3,2,1,0:T(8,128)} %first_stage.1.middle, f32[64,64,512]{2,1,0:T(8,128)} %scalar.9, f32[64,64,512]{2,1,0:T(8,128)} %prefactor.9, ...), custom_call_target="tpu_custom_call" | custom-call | flops 337379328 | bytes 18874368 | tf_op jit(solution)/shard_map/pallas_call | solution.py:455
  34.9 1.3 %collective-permute-start.3 = (f32[4,136,128]{2,1,0:T(8,128)}, f32[4,136,128]{2,1,0:T(8,128)S(1)}, u32[]{:S(2)}, u32[]{:S(2)}) collective-permute-start(f32[4,136,128]{2,1,0:T(8,128)} %get-tuple-element.20), channel_id=1, source_target_pairs={{4,0},{8,4},{12,8},{16,12},{20,16},{24,20},{28,24},{5,1},{9,5},{13... | collective-permute-start | bytes 835592 | tf_op jit(solution)/shard_map/ppermute | solution.py:491
  36.2 3.0 %collective-permute-start.2 = (f32[4,136,128]{2,1,0:T(8,128)}, f32[4,136,128]{2,1,0:T(8,128)S(1)}, u32[]{:S(2)}, u32[]{:S(2)}) collective-permute-start(f32[4,136,128]{2,1,0:T(8,128)} %get-tuple-element.19), channel_id=1, source_target_pairs={{0,4},{4,8},{8,12},{12,16},{16,20},{20,24},{24,28},{1,5},{5,9},{9,... | collective-permute-start | bytes 835592 | tf_op jit(solution)/shard_map/ppermute | solution.py:491
  39.2 1.5 %collective-permute-start.5 = (f32[2,64,512]{2,1,0:T(8,128)S(1)}, f32[2,64,512]{2,1,0:T(8,128)S(1)}, u32[]{:S(2)}, u32[]{:S(2)}) collective-permute-start(f32[2,64,512]{2,1,0:T(8,128)S(1)} %pad_maximum_fusion.3), channel_id=1, source_target_pairs={{0,8},{4,12},{8,0},{12,4},{16,24},{20,28},{24,16},{28,20},{1,9},{5... | collective-permute-start | bytes 786440 | tf_op jit(solution)/shard_map/ppermute | solution.py:495
  40.8 1.6 %collective-permute-start.9 = (f32[36,32,128]{2,1,0:T(8,128)}, f32[36,32,128]{2,1,0:T(8,128)S(1)}, u32[]{:S(2)}, u32[]{:S(2)}) collective-permute-start(f32[36,32,128]{2,1,0:T(8,128)} %get-tuple-element.27), channel_id=1, source_target_pairs={{0,1},{1,0},{2,3},{3,2},{4,5},{5,4},{6,7},{7,6},{8,9},{9,8},{10,11... | collective-permute-start | bytes 1769480 | tf_op jit(solution)/shard_map/ppermute | solution.py:495
  43.1 6.9 %shard_map.69 = (f32[64,64,512]{2,1,0:T(8,128)}, f32[20,32,128]{2,1,0:T(8,128)}, f32[20,32,128]{2,1,0:T(8,128)}) custom-call(f32[4,64,64,128]{3,2,1,0:T(8,128)} %first_stage.1.middle, f32[64,64,512]{2,1,0:T(8,128)} %scalar.9, f32[64,64,512]{2,1,0:T(8,128)} %prefactor.9, f32[2,4,64,128]{3,2,1,0:T(8,128)} %copy-done.1, ...), custom_call_target="tpu_custom_call", output_to_operand_aliasing={{0}: (8, {})} | custom-call | flops 187432960 | bytes 10485760 | tf_op jit(solution)/shard_map/pallas_call | solution.py:455
  50.8 4.7 %shard_map.70 = (f32[64,64,512]{2,1,0:T(8,128)}, f32[8,32,128]{2,1,0:T(8,128)}, f32[8,32,128]{2,1,0:T(8,128)}) custom-call(f32[4,64,64,128]{3,2,1,0:T(8,128)} %first_stage.1.middle, f32[64,64,512]{2,1,0:T(8,128)} %scalar.9, f32[64,64,512]{2,1,0:T(8,128)} %prefactor.9, f32[2,4,64,128]{3,2,1,0:T(8,128)} %copy-done.1, ...), custom_call_target="tpu_custom_call", output_to_operand_aliasing={{0}: (8, {})} | custom-call | flops 74973184 | bytes 4194304 | tf_op jit(solution)/shard_map/pallas_call | solution.py:455
  56.0 1.6 %collective-permute-start.11 = (f32[20,32,128]{2,1,0:T(8,128)S(1)}, f32[20,32,128]{2,1,0:T(8,128)S(1)}, u32[]{:S(2)}, u32[]{:S(2)}) collective-permute-start(f32[20,32,128]{2,1,0:T(8,128)S(1)} %copy-done.7), channel_id=1, source_target_pairs={{0,1},{1,0},{2,3},{3,2},{4,5},{5,4},{6,7},{7,6},{8,9},{9,8},{10,11... | collective-permute-start | bytes 983048 | tf_op jit(solution)/shard_map/ppermute | solution.py:495
  57.6 4.5 %collective-permute-done.7 = f32[8,32,128]{2,1,0:T(8,128)S(1)} collective-permute-done((f32[8,32,128]{2,1,0:T(8,128)}, f32[8,32,128]{2,1,0:T(8,128)S(1)}, u32[]{:S(2)}, u32[]{:S(2)}) %collective-permute-start.7) | collective-permute-done | bytes 131104 | tf_op jit(solution)/shard_map/ppermute | solution.py:495
  62.1 0.9 add.18
  63.8 0.8 pad_maximum_fusion.1
  64.6 1.2 collective-permute-start.6
  65.9 1.1 collective-permute-start.10
  67.1 3.7 %collective-permute-done.11 = f32[20,32,128]{2,1,0:T(8,128)S(1)} collective-permute-done((f32[20,32,128]{2,1,0:T(8,128)S(1)}, f32[20,32,128]{2,1,0:T(8,128)S(1)}, u32[]{:S(2)}, u32[]{:S(2)}) %collective-permute-start.11) | collective-permute-done | bytes 327712 | tf_op jit(solution)/shard_map/ppermute | solution.py:495
  71.6 18.6 %collective-permute-done.12 = f32[20,16,128]{2,1,0:T(8,128)S(1)} collective-permute-done((f32[20,16,128]{2,1,0:T(8,128)S(1)}, f32[20,16,128]{2,1,0:T(8,128)S(1)}, u32[]{:S(2)}, u32[]{:S(2)}) %collective-permute-start.12) | collective-permute-done | bytes 163872 | tf_op jit(solution)/shard_map/ppermute | solution.py:495
  90.5 0.9 pad_maximum_fusion.2
  91.4 3.8 %all-to-all-start = ((f32[8,64,256]{2,1,0:T(8,128)}), f32[8,64,256]{2,1,0:T(8,128)S(1)}, u32[]{:S(2)}, u32[]{:S(2)}) async-start(f32[8,64,256]{2,1,0:T(8,128)} %pad_maximum_fusion.2), calls=%async_computation | async-start | bytes 1048576 | tf_op jit(solution)/shard_map/all_to_all | solution.py:552
  95.7 9.1 %all-to-all-done = f32[8,64,256]{2,1,0:T(8,128)S(1)} async-done(((f32[8,64,256]{2,1,0:T(8,128)}), f32[8,64,256]{2,1,0:T(8,128)S(1)}, u32[]{:S(2)}, u32[]{:S(2)}) %all-to-all-start) | async-done | bytes 524320 | tf_op jit(solution)/shard_map/all_to_all | solution.py:552
  105.5 12.1 %all_to_all.10 = f32[8,64,256]{2,1,0:T(8,128)S(1)} all-to-all(f32[8,64,256]{2,1,0:T(8,128)S(1)} %fusion), channel_id=1, replica_groups=mesh['gx'=8,'gy'=4] {'gx'}, dimensions={0} | all-to-all | bytes 1048576 | tf_op jit(solution)/shard_map/all_to_all | solution.py:555
  (52 shorter events, 7.1 us)
Async XLA Ops:
  0.6 23.0 %collective-permute-start.4 = (f32[64,512]{1,0:T(8,128)}, f32[64,512]{1,0:T(8,128)S(1)}, u32[]{:S(2)}, u32[]{:S(2)}) collective-permute-start(f32[64,512]{1,0:T(8,128)} %param.7), channel_id=1, source_target_pairs={{0,16},{4,20},{8,24},{12,28},{16,0},{20,4},{24,8},{28,12},{1,17},{... | collective-permute-start | bytes 393224 | tf_op jit(solution)/shard_map/ppermute | solution.py:495
  7.7 16.0 %collective-permute-start.1 = (f32[2,4,64,128]{3,2,1,0:T(8,128)}, f32[2,4,64,128]{3,2,1,0:T(8,128)S(1)}, u32[]{:S(2)}, u32[]{:S(2)}) collective-permute-start(f32[2,4,64,128]{3,2,1,0:T(8,128)} %get-tuple-element.16.after), channel_id=1, source_target_pairs={{1,0},{2,1},{3,2},{5,4},{6,5},{7,6},{9,8},{10,9},{11,10},{13,12},{... | collective-permute-start | bytes 786440 | tf_op jit(solution)/shard_map/ppermute | solution.py:491
  9.0 14.7 %collective-permute-start = (f32[2,4,64,128]{3,2,1,0:T(8,128)}, f32[2,4,64,128]{3,2,1,0:T(8,128)S(1)}, u32[]{:S(2)}, u32[]{:S(2)}) collective-permute-start(f32[2,4,64,128]{3,2,1,0:T(8,128)} %get-tuple-element.17), channel_id=1, source_target_pairs={{0,1},{1,2},{2,3},{4,5},{5,6},{6,7},{8,9},{9,10},{10,11},{12,13},{... | collective-permute-start | bytes 786440 | tf_op jit(solution)/shard_map/ppermute | solution.py:491
  13.5 10.1 %copy-start.6 = (f32[64,512]{1,0:T(8,128)S(1)}, f32[64,512]{1,0:T(8,128)}, u32[]{:S(2)}) copy-start(f32[64,512]{1,0:T(8,128)} %param.7) | copy-start | bytes 393220
  23.6 0.7 copy-start
  23.7 0.8 copy-start.1
  34.9 7.5 %collective-permute-start.3 = (f32[4,136,128]{2,1,0:T(8,128)}, f32[4,136,128]{2,1,0:T(8,128)S(1)}, u32[]{:S(2)}, u32[]{:S(2)}) collective-permute-start(f32[4,136,128]{2,1,0:T(8,128)} %get-tuple-element.20), channel_id=1, source_target_pairs={{4,0},{8,4},{12,8},{16,12},{20,16},{24,20},{28,24},{5,1},{9,5},{13... | collective-permute-start | bytes 835592 | tf_op jit(solution)/shard_map/ppermute | solution.py:491
  36.2 13.9 %collective-permute-start.2 = (f32[4,136,128]{2,1,0:T(8,128)}, f32[4,136,128]{2,1,0:T(8,128)S(1)}, u32[]{:S(2)}, u32[]{:S(2)}) collective-permute-start(f32[4,136,128]{2,1,0:T(8,128)} %get-tuple-element.19), channel_id=1, source_target_pairs={{0,4},{4,8},{8,12},{12,16},{16,20},{20,24},{24,28},{1,5},{5,9},{9,... | collective-permute-start | bytes 835592 | tf_op jit(solution)/shard_map/ppermute | solution.py:491
  39.2 18.3 %collective-permute-start.5 = (f32[2,64,512]{2,1,0:T(8,128)S(1)}, f32[2,64,512]{2,1,0:T(8,128)S(1)}, u32[]{:S(2)}, u32[]{:S(2)}) collective-permute-start(f32[2,64,512]{2,1,0:T(8,128)S(1)} %pad_maximum_fusion.3), channel_id=1, source_target_pairs={{0,8},{4,12},{8,0},{12,4},{16,24},{20,28},{24,16},{28,20},{1,9},{5... | collective-permute-start | bytes 786440 | tf_op jit(solution)/shard_map/ppermute | solution.py:495
  40.8 25.0 %collective-permute-start.9 = (f32[36,32,128]{2,1,0:T(8,128)}, f32[36,32,128]{2,1,0:T(8,128)S(1)}, u32[]{:S(2)}, u32[]{:S(2)}) collective-permute-start(f32[36,32,128]{2,1,0:T(8,128)} %get-tuple-element.27), channel_id=1, source_target_pairs={{0,1},{1,0},{2,3},{3,2},{4,5},{5,4},{6,7},{7,6},{8,9},{9,8},{10,11... | collective-permute-start | bytes 1769480 | tf_op jit(solution)/shard_map/ppermute | solution.py:495
  42.3 0.7 copy-start.5
  50.0 0.7 copy-start.4
  50.7 5.3 %copy-start.7 = (f32[20,32,128]{2,1,0:T(8,128)S(1)}, f32[20,32,128]{2,1,0:T(8,128)}, u32[]{:S(2)}) copy-start(f32[20,32,128]{2,1,0:T(8,128)} %get-tuple-element.29) | copy-start | bytes 983044
  50.7 15.1 %copy-start.2 = (f32[36,32,128]{2,1,0:T(8,128)S(1)}, f32[36,32,128]{2,1,0:T(8,128)}, u32[]{:S(2)}) copy-start(f32[36,32,128]{2,1,0:T(8,128)} %get-tuple-element.26) | copy-start | bytes 1769476
  50.7 20.1 %copy-start.3 = (f32[20,32,128]{2,1,0:T(8,128)S(1)}, f32[20,32,128]{2,1,0:T(8,128)}, u32[]{:S(2)}) copy-start(f32[20,32,128]{2,1,0:T(8,128)} %get-tuple-element.28) | copy-start | bytes 983044
  55.5 6.6 %collective-permute-start.7 = (f32[8,32,128]{2,1,0:T(8,128)}, f32[8,32,128]{2,1,0:T(8,128)S(1)}, u32[]{:S(2)}, u32[]{:S(2)}) collective-permute-start(f32[8,32,128]{2,1,0:T(8,128)} %get-tuple-element.25), channel_id=1, source_target_pairs={{0,1},{1,0},{2,3},{3,2},{4,5},{5,4},{6,7},{7,6},{8,9},{9,8},{10,11... | collective-permute-start | bytes 393224 | tf_op jit(solution)/shard_map/ppermute | solution.py:495
  56.0 14.8 %collective-permute-start.11 = (f32[20,32,128]{2,1,0:T(8,128)S(1)}, f32[20,32,128]{2,1,0:T(8,128)S(1)}, u32[]{:S(2)}, u32[]{:S(2)}) collective-permute-start(f32[20,32,128]{2,1,0:T(8,128)S(1)} %copy-done.7), channel_id=1, source_target_pairs={{0,1},{1,0},{2,3},{3,2},{4,5},{5,4},{6,7},{7,6},{8,9},{9,8},{10,11... | collective-permute-start | bytes 983048 | tf_op jit(solution)/shard_map/ppermute | solution.py:495
  63.0 8.4 %collective-permute-start.8 = (f32[8,16,128]{2,1,0:T(8,128)S(1)}, f32[8,16,128]{2,1,0:T(8,128)S(1)}, u32[]{:S(2)}, u32[]{:S(2)}) collective-permute-start(f32[8,16,128]{2,1,0:T(8,128)S(1)} %slice.25), channel_id=1, source_target_pairs={{0,2},{1,3},{2,0},{3,1},{4,6},{5,7},{6,4},{7,5},{8,10},{9,11},{10,... | collective-permute-start | bytes 196616 | tf_op jit(solution)/shard_map/ppermute | solution.py:495
  64.6 30.5 %collective-permute-start.6 = (f32[2,2,64,512]{3,2,1,0:T(8,128)}, f32[2,2,64,512]{3,2,1,0:T(8,128)S(1)}, u32[]{:S(2)}, u32[]{:S(2)}) collective-permute-start(f32[2,2,64,512]{3,2,1,0:T(8,128)} %pad_maximum_fusion.1), channel_id=1, source_target_pairs={{0,4},{4,0},{8,12},{12,8},{16,20},{20,16},{24,28},{28,24},{1,5},{5... | collective-permute-start | bytes 1572872 | tf_op jit(solution)/shard_map/ppermute | solution.py:495
  65.9 24.3 %collective-permute-start.10 = (f32[36,16,128]{2,1,0:T(8,128)S(1)}, f32[36,16,128]{2,1,0:T(8,128)S(1)}, u32[]{:S(2)}, u32[]{:S(2)}) collective-permute-start(f32[36,16,128]{2,1,0:T(8,128)S(1)} %slice.27), channel_id=1, source_target_pairs={{0,2},{1,3},{2,0},{3,1},{4,6},{5,7},{6,4},{7,5},{8,10},{9,11},{10,... | collective-permute-start | bytes 884744 | tf_op jit(solution)/shard_map/ppermute | solution.py:495
  70.9 19.3 %collective-permute-start.12 = (f32[20,16,128]{2,1,0:T(8,128)S(1)}, f32[20,16,128]{2,1,0:T(8,128)S(1)}, u32[]{:S(2)}, u32[]{:S(2)}) collective-permute-start(f32[20,16,128]{2,1,0:T(8,128)S(1)} %slice.29), channel_id=1, source_target_pairs={{0,2},{1,3},{2,0},{3,1},{4,6},{5,7},{6,4},{7,5},{8,10},{9,11},{10,... | collective-permute-start | bytes 491528 | tf_op jit(solution)/shard_map/ppermute | solution.py:495
  91.4 13.5 %all-to-all-start = ((f32[8,64,256]{2,1,0:T(8,128)}), f32[8,64,256]{2,1,0:T(8,128)S(1)}, u32[]{:S(2)}, u32[]{:S(2)}) async-start(f32[8,64,256]{2,1,0:T(8,128)} %pad_maximum_fusion.2), calls=%async_computation | async-start | bytes 1048576 | tf_op jit(solution)/shard_map/all_to_all | solution.py:552
